TPU v7x, 32 devices: a whole 2x2x4 slice. The times are simulated.
32 devices in a mesh: dom: 8 (over z, x), group: 4 (over y, core).
Axes of the slice: x: 2, y: 2, z: 4, core: 2. Of those that a mesh axis runs over, the one named last changes fastest.
Arguments:
- features: bfloat16 [65536, 256], P(('dom', 'group')), may hold values from -6 to 6
- boundary: int32 [2048], P(('dom', 'group')), may hold values from 0 to 127, as said below
- request: int32 [128, 24], P(('dom', 'group')), may hold values from 0 to 63, as said below
- tile_slots: int32 [512, 8], P(('dom', 'group')), may hold values from 0 to 223, as said below
- neighbors: int32 [65536, 10], P(('dom', 'group')), may hold values from 0 to 127
- negatives: int32 [65536, 4], P(('dom', 'group')), may hold values from 0 to 127
- layer_weight: bfloat16 [512, 256], replicated, may hold values from -0.25 to 0.25
Outputs:
- feature_grad: float32 [65536, 256], P(('dom', 'group'))
- weight_grad: float32 [512, 256], replicated
- loss_mean: float32 [], replicated
Inputs may be any that keep to these rules, and one draw needn't show every extreme that they name: The 64 entries boundary[i * 64 to i * 64 + 63] are distinct numbers of device i's own row blocks. `request`: row i * 4 + e holds 24 distinct positions in the boundary list of device (i // 4) * 4 + e. `tile_slots`: entries are numbers s as in the first step; the 128 entries of one device are distinct and include every number from 128 to 223.
All inputs are finite; a program needn't handle non-finite values.
Results may differ from a plain program's by a relative error of at most 0.00075.
The roundings to bfloat16 on the way count: a program that leaves them out, or rounds other values in their place, can miss the bound.
Values may be sent and summed in bfloat16 or wider, within the bound.
No kernel may reach another device: no remote copies, remote signals or barrier semaphores. Data moves between devices by JAX's collectives and lax.ppermute only.
A program may use at most 64 MiB of HBM per device.

v0:
```python
import jax
import jax.numpy as jnp
from jax import lax
from jax.sharding import PartitionSpec as P

TILE = 128
BLK = 16
NBT = 8
DEG = 10
NNEG = 4


margin = 0.5
epsilon = 1e-06


def contract(form, left, right):
    return jnp.einsum(form, left, right, preferred_element_type=jnp.float32)


def tile_terms(own_rows, candidates, neighbor_ids, negative_ids, layer_weight):
    tile_count, tile_rows, feature_width = own_rows.shape
    cand_count = candidates.shape[1]
    degree = neighbor_ids.shape[-1]
    negative_count = negative_ids.shape[-1]
    slot_ids = jnp.arange(cand_count, dtype=jnp.int32)
    counts = jnp.sum((neighbor_ids[..., None] == slot_ids).astype(jnp.float32), axis=2).astype(
        jnp.bfloat16
    )
    aggregate = (contract("tuc,tcd->tud", counts, candidates) / degree).astype(jnp.bfloat16)
    joined = jnp.concatenate([own_rows, aggregate], axis=-1).reshape(-1, 2 * feature_width)
    preact = jnp.dot(joined, layer_weight, preferred_element_type=jnp.float32)
    gate_value = jax.nn.sigmoid(preact)
    hidden = preact * gate_value
    norm_scale = lax.rsqrt(jnp.mean(hidden * hidden, axis=-1, keepdims=True) + epsilon)
    embedding = hidden * norm_scale
    embed_half = embedding.astype(jnp.bfloat16).reshape(tile_count, tile_rows, feature_width)
    inv_root = feature_width ** (-0.5)
    scores = contract("tud,tcd->tuc", embed_half, candidates) * inv_root
    positive = (neighbor_ids[..., 0:1] == slot_ids).astype(jnp.float32)
    negative = (negative_ids[..., None] == slot_ids).astype(jnp.float32)
    pos_score = jnp.sum(scores * positive, axis=-1, keepdims=True)
    neg_score = jnp.sum(scores[:, :, None, :] * negative, axis=-1)
    excess = margin + neg_score - pos_score
    loss_sum = jnp.sum(jax.nn.softplus(excess)) / negative_count
    neg_weight = jax.nn.sigmoid(excess) / negative_count
    dscores = (
        jnp.sum(neg_weight[..., None] * negative, axis=2)
        - jnp.sum(neg_weight, axis=-1, keepdims=True) * positive
    ) * inv_root
    dscores_half = dscores.astype(jnp.bfloat16)
    dembedding = contract("tuc,tcd->tud", dscores_half, candidates).reshape(-1, feature_width)
    dcandidates = contract("tuc,tud->tcd", dscores_half, embed_half)
    dhidden = norm_scale * (
        dembedding - embedding * jnp.mean(dembedding * embedding, axis=-1, keepdims=True)
    )
    dpreact = (dhidden * gate_value * (1.0 + preact * (1.0 - gate_value))).astype(jnp.bfloat16)
    dweight = jnp.dot(joined.T, dpreact, preferred_element_type=jnp.float32)
    dinputs = jnp.dot(dpreact, layer_weight.T, preferred_element_type=jnp.float32)
    dself = dinputs[:, :feature_width].reshape(tile_count, tile_rows, feature_width)
    daggregate = (
        (dinputs[:, feature_width:] / degree)
        .astype(jnp.bfloat16)
        .reshape(tile_count, tile_rows, feature_width)
    )
    dcandidates = dcandidates + contract("tuc,tud->tcd", counts, daggregate)
    return (loss_sum, dweight, dself, dcandidates)


def per_device(features, boundary, request, tile_slots, neighbors, negatives, layer_weight):
    row_count, feature_width = features.shape
    peer_count = lax.axis_size("group")
    capacity = request.shape[1]
    bound_count = boundary.shape[0]
    block_count = row_count // BLK
    tile_count = tile_slots.shape[0]
    blocks = features.reshape(block_count, BLK, feature_width)
    shared = blocks[boundary].reshape(bound_count * BLK, feature_width)
    published = lax.all_gather(shared, "group", axis=0, tiled=True).reshape(
        peer_count, bound_count, BLK, feature_width
    )
    received = published[jnp.arange(peer_count, dtype=jnp.int32)[:, None], request]
    table_rows = jnp.concatenate(
        [blocks, received.reshape(peer_count * capacity, BLK, feature_width)], axis=0
    )
    slot_list = tile_slots.reshape(-1)
    candidates = table_rows[slot_list].reshape(tile_count, NBT * BLK, feature_width)
    own_rows = features.reshape(tile_count, TILE, feature_width)
    neighbor_ids = neighbors.reshape(tile_count, TILE, DEG)
    negative_ids = negatives.reshape(tile_count, TILE, NNEG)
    loss_sum, dweight, dself, dcandidates = tile_terms(
        own_rows, candidates, neighbor_ids, negative_ids, layer_weight
    )
    table_grad = jnp.zeros((block_count + peer_count * capacity, BLK, feature_width), jnp.float32)
    table_grad = table_grad.at[slot_list].add(dcandidates.reshape(-1, BLK, feature_width))
    own_grad = table_grad[:block_count] + dself.reshape(block_count, BLK, feature_width)
    incoming = table_grad[block_count:]
    sectioned = jnp.zeros((peer_count, bound_count, BLK, feature_width), jnp.float32)
    sectioned = sectioned.at[jnp.arange(peer_count, dtype=jnp.int32)[:, None], request].add(
        incoming.reshape(peer_count, capacity, BLK, feature_width)
    )
    summed_back = lax.psum_scatter(
        sectioned.reshape(peer_count * bound_count * BLK, feature_width),
        "group",
        scatter_dimension=0,
        tiled=True,
    )
    own_grad = own_grad.at[boundary].add(summed_back.reshape(bound_count, BLK, feature_width))
    totals = lax.psum((dweight, loss_sum), ("dom", "group"))
    device_total = lax.axis_size(("dom", "group"))
    return (
        own_grad.reshape(row_count, feature_width),
        totals[0] / row_count,
        totals[1] / (row_count * device_total),
    )


def solution(mesh):
    return jax.shard_map(
        per_device,
        mesh=mesh,
        in_specs=(
            P(("dom", "group"), None),
            P(("dom", "group")),
            P(("dom", "group"), None),
            P(("dom", "group"), None),
            P(("dom", "group"), None),
            P(("dom", "group"), None),
            P(),
        ),
        out_specs=(P(("dom", "group"), None), P(), P()),
        check_vma=False,
    )
```

profile of v0, /device:TPU:0, one launch (start us, length us, event | category | flops | bytes accessed | tf_op | source)
XLA Modules:
  0.0 263.6 jit_solution(1300090860702294701)
XLA Ops:
  7.9 2.7 %gather_fusion = bf16[64,16,256]{2,1,0:T(8,128)(2,1)} fusion(bf16[128,16,256]{2,1,0:T(8,128)(2,1)} %bitcast.70, s32[1024]{0:T(1024)S(1)} %pad_clamp_fusion.1), kind=kCustom, calls=%fused_computation | custom fusion | bytes 1048832 | tf_op jit(solution)/shard_map/gather | solution.py:78
  13.4 4.0 %convert_reduce_fusion = bf16[16,128,128]{2,1,0:T(8,128)(2,1)S(1)} fusion(s32[16,128,10]{1,2,0:T(8,128)S(1)} %copy.24), kind=kLoop, calls=%fused_computation.6 | loop fusion | flops 7602176 | bytes 606208 | tf_op jit(solution)/shard_map/reduce_sum | solution.py:27
  17.5 18.7 %all-gather.2.cloned.1.call-done = bf16[4096,256]{1,0:T(8,128)(2,1)} async-done(((bf16[1024,256]{1,0:T(8,128)(2,1)}), bf16[4096,256]{1,0:T(8,128)(2,1)}) %all-gather.2.cloned.1.call-update) | async-done | bytes 2097168 | tf_op jit(solution)/shard_map/all_gather | solution.py:79
  36.2 2.6 gather_fusion.1
  38.8 1.4 pad_maximum_fusion.1
  40.2 2.1 gather_fusion.2
  43.5 1.1 multiply_reduce_fusion
  45.3 1.0 copy-done.5
  46.3 1.4 select_reduce_fusion.2
  47.7 2.5 copy.25
  50.3 3.9 %select_reduce_fusion.1 = f32[16,128,4]{1,2,0:T(4,128)S(1)} fusion(f32[16,128,128]{2,1,0:T(8,128)} %copy.25, s32[16,128,4]{1,2,0:T(4,128)S(1)} %bitcast.78), kind=kLoop, calls=%fused_computation.9 | loop fusion | flops 3137536 | bytes 1114112 | tf_op jit(solution)/shard_map/reduce_sum | solution.py:43
  54.8 3.8 %select_reduce_fusion = f32[16,128,128]{2,1,0:T(8,128)} fusion(f32[16,128,4]{1,2,0:T(4,128)S(1)} %get-tuple-element.4, s32[16,128,4]{1,2,0:T(4,128)S(1)} %bitcast.79), kind=kLoop, calls=%fused_computation.8 | loop fusion | flops 2883584 | bytes 1114112 | tf_op jit(solution)/shard_map/reduce_sum | solution.py:48
  58.6 2.5 copy.27
  61.1 1.9 fusion.12
  63.0 1.7 fusion.13
  64.7 1.0 fusion.1
  65.8 1.4 fusion.5
  67.3 1.5 fusion.7
  68.8 2.7 %fusion.27 = f32[2048,512]{1,0:T(8,128)} fusion(bf16[2048,256]{1,0:T(8,128)(2,1)S(1)} %fusion.5, bf16[512,256]{1,0:T(8,128)(2,1)S(1)} %copy-done), kind=kOutput, calls=%fused_computation.70 | convolution fusion | flops 536870912 | bytes 5505024 | tf_op jit(solution)/shard_map/dot_general | solution.py:59
  71.8 2.7 %fusion = (bf16[2048,256]{1,0:T(8,128)(2,1)S(1)}, f32[2048,256]{1,0:T(8,128)S(1)}) fusion(f32[2048,512]{1,0:T(8,128)} %fusion.27), kind=kLoop, calls=%fused_computation.13 | loop fusion | flops 1048576 | bytes 7340032 | tf_op jit(solution)/shard_map/convert_element_type | solution.py:63
  74.7 1.8 convolution_add_fusion
  76.5 2.3 broadcast_in_dim.10
  78.8 17.5 %scatter_fusion = f32[224,16,256]{2,1,0:T(8,128)} fusion(f32[224,16,256]{2,1,0:T(8,128)} %broadcast_in_dim.10, s32[128]{0:T(128)S(1)} %fusion.19, f32[128,16,256]{2,1,0:T(8,128)} %bitcast.65), kind=kCustom, calls=%fused_computation.3 | custom fusion | flops 524288 | bytes 6291968 | tf_op jit(solution)/shard_map/scatter-add | solution.py:95
  96.2 2.7 %slice.32 = f32[96,16,256]{2,1,0:T(8,128)} slice(f32[224,16,256]{2,1,0:T(8,128)} %scatter_fusion), slice={[128:224], [0:16], [0:256]} | slice | bytes 3145728 | tf_op jit(solution)/shard_map/slice | solution.py:97
  98.9 2.5 broadcast_in_dim.14
  101.4 14.0 %scatter_fusion.1 = f32[4,64,16,256]{3,2,1,0:T(8,128)} fusion(f32[4,64,16,256]{3,2,1,0:T(8,128)} %broadcast_in_dim.14, s32[96]{0:T(128)S(1)} %reshape.154, f32[96,16,256]{2,1,0:T(8,128)} %slice.32), kind=kCustom, calls=%fused_computation.4 | custom fusion | flops 393216 | bytes 4719360 | tf_op jit(solution)/shard_map/scatter-add | solution.py:99
  116.0 39.4 %psum.15 = f32[]{:T(128)} all-reduce(f32[]{:T(128)S(6)} %div.58), channel_id=1, replica_groups=mesh['dom'=8,'group'=4] {'dom','group'}, use_global_device_ids=true, to_apply=%region_13.14 | all-reduce | flops 1 | bytes 8 | tf_op jit(solution)/shard_map/psum | solution.py:109
  156.0 3.4 %slice_add_fusion = f32[128,16,256]{2,1,0:T(8,128)} fusion(f32[128,16,256]{2,1,0:T(8,128)S(1)} %bitcast.64, f32[224,16,256]{2,1,0:T(8,128)} %scatter_fusion), kind=kLoop, calls=%fused_computation.11 | loop fusion | flops 524288 | bytes 6291456 | tf_op jit(solution)/shard_map/add | solution.py:96
  159.4 41.4 %all-reduce.2.cloned.1.call-done = f32[512,256]{1,0:T(8,128)} async-done(((f32[512,256]{1,0:T(8,128)}), f32[512,256]{1,0:T(8,128)}) %all-reduce.2.cloned.1.call-update) | async-done | bytes 524304 | tf_op jit(solution)/shard_map/psum | solution.py:109
  200.8 1.9 broadcast_multiply_fusion
  202.6 44.3 %reduce-scatter.2.cloned.1.call-done = f32[1024,256]{1,0:T(8,128)} async-done(((f32[4096,256]{1,0:T(8,128)}), f32[1024,256]{1,0:T(8,128)}) %reduce-scatter.2.cloned.1.call-update) | async-done | bytes 1048592 | tf_op jit(solution)/shard_map/reduce_scatter | solution.py:102
  246.9 9.0 %scatter_fusion.2 = f32[128,16,256]{2,1,0:T(8,128)} fusion(f32[128,16,256]{2,1,0:T(8,128)} %slice_add_fusion, s32[64]{0:T(128)S(1)} %compare_select_fusion.2, f32[64,16,256]{2,1,0:T(8,128)} %bitcast.75), kind=kCustom, calls=%fused_computation.5 | custom fusion | flops 262144 | bytes 3145984 | tf_op jit(solution)/shard_map/scatter-add | solution.py:108
  (49 shorter events, 6.5 us)
Async XLA Ops:
  7.2 35.6 %copy-start = (bf16[512,256]{1,0:T(8,128)(2,1)S(1)}, bf16[512,256]{1,0:T(8,128)(2,1)}, u32[]{:S(2)}) copy-start(bf16[512,256]{1,0:T(8,128)(2,1)} %param.13) | copy-start | bytes 786436
  7.2 29.0 %all-gather.2.cloned.1.call-start = ((), (), s32[]{:S(2)}) async-start(), calls=%async_computation.1 | async-start | bytes 2621440 | tf_op jit(solution)/shard_map/all_gather | solution.py:79
  7.9 30.8 %copy-start.7 = (bf16[2048,256]{1,0:T(8,128)(2,1)S(1)}, bf16[2048,256]{1,0:T(8,128)(2,1)}, u32[]{:S(2)}) copy-start(bf16[2048,256]{1,0:T(8,128)(2,1)} %param.7) | copy-start | bytes 3145732
  10.7 190.1 %all-reduce.2.cloned.1.call-start = ((), (), s32[]{:S(2)}) async-start(), calls=%async_computation.3 | async-start | bytes 1048576 | tf_op jit(solution)/shard_map/psum | solution.py:109
  17.5 24.9 %copy-start.3 = (bf16[16,128,128]{2,1,0:T(8,128)(2,1)}, bf16[16,128,128]{2,1,0:T(8,128)(2,1)S(1)}, u32[]{:S(2)}) copy-start(bf16[16,128,128]{2,1,0:T(8,128)(2,1)S(1)} %convert_reduce_fusion) | copy-start | bytes 1572868
  42.3 1.2 copy-start.8
  42.8 1.9 copy-start.10
  45.3 1.0 copy-start.5
  46.3 4.0 %copy-start.12 = (s32[2048,4]{0,1:T(4,128)S(1)}, s32[2048,4]{0,1:T(4,128)}, u32[]{:S(2)}) copy-start(s32[2048,4]{0,1:T(4,128)} %param.12) | copy-start | bytes 98308
  61.1 1.9 copy-start.1
  61.1 1.9 copy-start.6
  65.7 1.5 copy-start.9
  65.8 1.5 copy-start.11
  71.5 3.0 %copy-start.4 = (bf16[16,128,128]{2,1,0:T(8,128)(2,1)S(1)}, bf16[16,128,128]{2,1,0:T(8,128)(2,1)}, u32[]{:S(2)}) copy-start(bf16[16,128,128]{2,1,0:T(8,128)(2,1)} %copy-done.3) | copy-start | bytes 1572868
  71.5 175.4 %reduce-scatter.2.cloned.1.call-start = ((), (), s32[]{:S(2)}) async-start(), calls=%async_computation.2 | async-start | bytes 5242880 | tf_op jit(solution)/shard_map/reduce_scatter | solution.py:102
  71.8 2.9 %copy-start.2 = (f32[16,128,256]{2,1,0:T(8,128)S(1)}, f32[16,128,256]{2,1,0:T(8,128)}, u32[]{:S(2)}) copy-start(f32[16,128,256]{2,1,0:T(8,128)} %fusion.13) | copy-start | bytes 6291460
Sparse Core Ops, SparseCore 0:
  10.8 25.3 all-gather.1
  71.6 129.0 all-reduce.1
  203.3 43.5 reduce-scatter.1
where the time goes:
time: 265 us; the launch traced here: 264 us
  waiting for transfers between devices  104 us (39%)
  other arithmetic  66.5 us (25%)
  blocking collectives  39.4 us (15%)
  local copies, waits for them, and re-layouts  24 us (9%)
  between operations  16.5 us (6%)
  matrix products  12.6 us (5%)
    reduce_scatter x1, waiting for transfers between devices, per_device(): lax.psum_scatter(sectioned.reshape(peer_count * bound_count * BLK, featur...  44.3 us
    psum x1, waiting for transfers between devices, per_device(): totals = lax.psum((dweight, loss_sum), ('dom', 'group'))  41.4 us
    psum x1, blocking collectives, per_device(): totals = lax.psum((dweight, loss_sum), ('dom', 'group'))  39.4 us
    all_gather x1, waiting for transfers between devices, per_device(): lax.all_gather(shared, 'group', axis=0, tiled=True)  18.7 us
    scatter-add x1, other arithmetic, per_device(): table_grad.at[slot_list].add(dcandidates.reshape(-1, BLK, feature_width))  17.5 us
    scatter-add x1, other arithmetic, per_device(): sectioned.at[jnp.arange(peer_count, dtype=jnp.int32)[:, None], request]  14 us
    scatter-add x1, other arithmetic, per_device(): own_grad.at[boundary]  9 us
    dot_general x5, matrix products, contract(): return jnp.einsum(form, left, right, preferred_element_type=jnp.float32)  7.26 us
  transfers between devices with their start and end apart: 3, of which 3 were waited for; matrix products, arithmetic and copies ran while one was open for 21% of the time, Pallas kernels for 0%

commit v1 on v0

v1 whole, which is shorter than its diff:
```python
import functools

import jax
import jax.numpy as jnp
from jax import lax
from jax.experimental import pallas as pl
from jax.experimental.pallas import tpu as pltpu
from jax.sharding import PartitionSpec as P

TILE = 128
BLK = 16
NBT = 8
PAD = 8
CHUNK = 4

margin = 0.5
epsilon = 1e-06

VMEM = pl.BlockSpec(memory_space=pltpu.VMEM)
SMEM = pl.BlockSpec(memory_space=pltpu.SMEM)
f32 = jnp.float32
bf16 = jnp.bfloat16


def dot(left, right, dims):
    return lax.dot_general(left, right, (dims, ((), ())), preferred_element_type=f32)


def call(kernel, out_shape, args, specs, out_specs, scratch=(), flops=0, name=None):
    size = sum(a.size * a.dtype.itemsize for a in args)
    return pl.pallas_call(
        kernel,
        out_shape=out_shape,
        in_specs=specs,
        out_specs=out_specs,
        scratch_shapes=list(scratch),
        cost_estimate=pl.CostEstimate(flops=flops, bytes_accessed=size, transcendentals=0),
        name=name,
    )(*args)


def share_kernel(boundary, request, feat, out):
    count = boundary.shape[0]

    def body(i, carry):
        out[i] = feat[boundary[i]]
        return carry

    lax.fori_loop(0, count, body, 0, unroll=8)
    rows, cols = request.shape
    row_ids = lax.broadcasted_iota(jnp.int32, (BLK, 128), 0)
    lane_ids = lax.broadcasted_iota(jnp.int32, (BLK, 128), 1)
    tag = jnp.zeros((BLK, 128), f32)
    for r in range(rows):
        for c in range(cols):
            tag = jnp.where((row_ids == r) & (lane_ids == c), request[r, c].astype(f32), tag)
    out[count] = jnp.zeros((BLK, feat.shape[2]), bf16)
    out[count, :, 0:128] = tag.astype(bf16)


def early_kernel(feat, weight, nbr, counts, pre):
    rows, width = feat.shape
    degree = nbr.shape[0]
    cand_ids = lax.broadcasted_iota(jnp.int32, (TILE, TILE), 0)
    top = weight[0:width, :]

    def body(t, carry):
        at = pl.ds(pl.multiple_of(t * TILE, TILE), TILE)
        ids = nbr[:, at]
        total = jnp.zeros((TILE, TILE), f32)
        for j in range(degree):
            total = total + jnp.where(ids[j : j + 1, :] == cand_ids, 1.0, 0.0)
        counts[at, :] = total.astype(bf16)
        return carry

    lax.fori_loop(0, rows // TILE, body, 0)
    step = CHUNK * TILE

    def dense(c, carry):
        at = pl.ds(pl.multiple_of(c * step, step), step)
        pre[at, :] = dot(feat[at, :], top, ((1,), (0,)))
        return carry

    lax.fori_loop(0, rows // step, dense, 0)


def main_kernel(peers, slots, request, boundary, feat3, feat, weight, nbr, neg, pre, counts, *rest):
    pieces = rest[: peers - 1]
    own, keep, send = rest[peers - 1 : peers + 2]
    back = rest[peers + 2 : 2 * peers + 1]
    cand, agg, dpre, dcand, where_own, where_slot, wgrad, losses = rest[2 * peers + 1 :]
    rows, width = feat.shape
    blocks = feat3.shape[0]
    capacity = request.shape[1]
    degree = nbr.shape[0]
    negs = neg.shape[0]
    me = lax.axis_index("group")

    def gather(i, carry):
        t = i // NBT
        s = slots[i - t * NBT, t]
        local = s < blocks
        r = jnp.maximum(s - blocks, 0)
        e = r // capacity
        at = request[e, r - e * capacity]
        k = e ^ me
        mine = local | (k == 0)
        own_at = jnp.where(local, jnp.minimum(s, blocks - 1), boundary[at])
        where_own[i] = jnp.where(mine, own_at, -1)

        @pl.when(jnp.logical_not(local))
        def _():
            where_slot[r] = i

        value = feat3[own_at]
        for p in range(1, peers):
            value = jnp.where(jnp.logical_not(mine) & (k == p), pieces[p - 1][at], value)
        cand[i] = value
        return carry

    lax.fori_loop(0, blocks, gather, 0)
    losses[...] = jnp.zeros(losses.shape, f32)
    top = weight[0:width, :]
    low = weight[width : 2 * width, :]
    cand_ids = lax.broadcasted_iota(jnp.int32, (TILE, TILE), 0)
    step = CHUNK * TILE
    inv_root = width ** (-0.5)

    def chunk(c, carry):
        at = pl.ds(pl.multiple_of(c * step, step), step)
        tiles = []
        for tt in range(CHUNK):
            t = c * CHUNK + tt
            cd = cand[pl.ds(t * NBT, NBT)].reshape(TILE, width)
            ct = counts[pl.ds(pl.multiple_of(t * TILE, TILE), TILE), :]
            tiles.append((cd, ct))
            part = (dot(ct, cd, ((0,), (0,))) / degree).astype(bf16)
            agg[pl.ds(pl.multiple_of(t * TILE, TILE), TILE), :] = part
        preact = pre[at, :] + dot(agg[at, :], low, ((1,), (0,)))
        gate = jax.nn.sigmoid(preact)
        hidden = preact * gate
        scale = lax.rsqrt(jnp.mean(hidden * hidden, axis=-1, keepdims=True) + epsilon)
        embedding = hidden * scale
        half = embedding.astype(bf16)
        demb = []
        dsc = []
        for tt in range(CHUNK):
            t = c * CHUNK + tt
            lanes = pl.ds(pl.multiple_of(t * TILE, TILE), TILE)
            cd, ct = tiles[tt]
            scores = dot(cd, half[tt * TILE : (tt + 1) * TILE, :], ((1,), (1,))) * inv_root
            first = nbr[:, lanes][0:1, :] == cand_ids
            ids = neg[:, lanes]
            hits = [ids[n : n + 1, :] == cand_ids for n in range(negs)]
            pos = jnp.sum(jnp.where(first, scores, 0.0), axis=0, keepdims=True)
            picked = jnp.concatenate(
                [jnp.sum(jnp.where(h, scores, 0.0), axis=0, keepdims=True) for h in hits], axis=0
            )
            excess = margin + picked - pos
            soft = jnp.maximum(excess, 0.0) + jnp.log1p(jnp.exp(-jnp.abs(excess)))
            losses[0:negs, :] += soft
            weights = jax.nn.sigmoid(excess) / negs
            total = jnp.sum(weights, axis=0, keepdims=True)
            ds = jnp.zeros((TILE, TILE), f32)
            for n in range(negs):
                ds = ds + jnp.where(hits[n], weights[n : n + 1, :], 0.0)
            ds = ((ds - jnp.where(first, total, 0.0)) * inv_root).astype(bf16)
            dsc.append(ds)
            demb.append(dot(ds, cd, ((0,), (0,))))
        demb = jnp.concatenate(demb, axis=0)
        mean = jnp.mean(demb * embedding, axis=-1, keepdims=True)
        dhidden = scale * (demb - embedding * mean)
        dp = (dhidden * gate * (1.0 + preact * (1.0 - gate))).astype(bf16)
        dpre[at, :] = dp
        own[pl.ds(c * (step // BLK), step // BLK)] = dot(dp, top, ((1,), (1,))).reshape(
            step // BLK, BLK, width
        )
        dagg = (dot(dp, low, ((1,), (1,))) / degree).astype(bf16)
        for tt in range(CHUNK):
            t = c * CHUNK + tt
            cd, ct = tiles[tt]
            part = slice(tt * TILE, (tt + 1) * TILE)
            got = dot(dsc[tt], half[part, :], ((1,), (0,))) + dot(ct, dagg[part, :], ((1,), (0,)))
            dcand[pl.ds(t * NBT, NBT)] = got.reshape(NBT, BLK, width)
        return carry

    lax.fori_loop(0, rows // step, chunk, 0)

    wgrad[0:width, :] = dot(feat[...], dpre[...], ((0,), (0,)))
    wgrad[width : 2 * width, :] = dot(agg[...], dpre[...], ((0,), (0,)))
    half_rows = width
    core = me & 1
    keep[0:half_rows, :] = wgrad[pl.ds(pl.multiple_of(core * half_rows, half_rows), half_rows), :]
    send[0:half_rows, :] = wgrad[
        pl.ds(pl.multiple_of((1 - core) * half_rows, half_rows), half_rows), :
    ]
    loss = jnp.sum(losses[...]) / negs
    spread = jnp.full((PAD, width), loss, f32)
    keep[half_rows : half_rows + PAD, :] = spread
    send[half_rows : half_rows + PAD, :] = spread

    def scatter(i, carry):
        d = where_own[i]
        to = jnp.maximum(d, 0)
        own[to] = own[to] + jnp.where(d >= 0, dcand[i], 0.0)
        return carry

    lax.fori_loop(0, blocks, scatter, 0, unroll=4)
    for k in range(1, peers):
        base = (me ^ k) * capacity

        def outgo(c, carry, k=k, base=base):
            back[k - 1][c] = dcand[where_slot[base + c]]
            return carry

        lax.fori_loop(0, capacity, outgo, 0, unroll=4)


def return_kernel(boundary, asked, own_in, *rest):
    grads, own = rest[:-1], rest[-1]
    own[...] = own_in[...]
    capacity = asked.shape[1]
    for k, got in enumerate(grads):

        def body(c, carry, k=k, got=got):
            to = boundary[asked[k, c]]
            own[to] = own[to] + got[c]
            return carry

        lax.fori_loop(0, capacity, body, 0, unroll=4)


def finish_kernel(rows, nodes, mine, other, wgrad, loss):
    half_rows = mine.shape[0] - PAD
    core = lax.axis_index("group") & 1
    wgrad[pl.ds(pl.multiple_of(core * half_rows, half_rows), half_rows), :] = (
        mine[0:half_rows, :] / rows
    )
    wgrad[pl.ds(pl.multiple_of((1 - core) * half_rows, half_rows), half_rows), :] = (
        other[0:half_rows, :] / rows
    )
    first = jnp.where(core == 0, mine[half_rows:, 0:128], other[half_rows:, 0:128])
    loss[0, 0] = jnp.max(first) / nodes


def per_device(features, boundary, request, tile_slots, neighbors, negatives, layer_weight):
    row_count, width = features.shape
    peers = lax.axis_size("group")
    domains = lax.axis_size("dom")
    devices = peers * domains
    capacity = request.shape[1]
    bound_count = boundary.shape[0]
    block_count = row_count // BLK
    blocks = features.reshape(block_count, BLK, width)
    nbr = neighbors.T
    neg = negatives.T
    slots = tile_slots.T
    sds = jax.ShapeDtypeStruct

    shared = call(
        share_kernel,
        sds((bound_count + 1, BLK, width), bf16),
        (boundary, request, blocks),
        [SMEM, SMEM, VMEM],
        VMEM,
        name="share",
    )
    pieces = {0: shared}
    bit = peers // 2
    while bit:
        for k in list(pieces):
            pairs = [(i, i ^ bit) for i in range(peers)]
            pieces[k | bit] = lax.ppermute(pieces[k], "group", pairs)
        bit //= 2

    counts, pre = call(
        early_kernel,
        (sds((row_count, TILE), bf16), sds((row_count, width), f32)),
        (features, layer_weight, nbr),
        [VMEM] * 3,
        (VMEM, VMEM),
        flops=2 * row_count * width * width * 8,
        name="early",
    )
    outs = call(
        functools.partial(main_kernel, peers),
        (
            sds((block_count, BLK, width), f32),
            sds((width + PAD, width), f32),
            sds((width + PAD, width), f32),
        )
        + (sds((capacity, BLK, width), f32),) * (peers - 1),
        (slots, request, boundary, blocks, features, layer_weight, nbr, neg, pre, counts)
        + tuple(pieces[k] for k in range(1, peers)),
        [SMEM] * 3 + [VMEM] * (6 + peers),
        (VMEM,) * (peers + 2),
        scratch=(
            pltpu.VMEM((block_count, BLK, width), bf16),
            pltpu.VMEM((row_count, width), bf16),
            pltpu.VMEM((row_count, width), bf16),
            pltpu.VMEM((block_count, BLK, width), f32),
            pltpu.SMEM((block_count,), jnp.int32),
            pltpu.SMEM((peers * capacity,), jnp.int32),
            pltpu.VMEM((2 * width, width), f32),
            pltpu.VMEM((8, TILE), f32),
        ),
        flops=2 * row_count * width * width * 20,
        name="main",
    )
    own, keep, send = outs[:3]
    back = outs[3:]

    everyone = ("dom", "group")

    def swap(x, masks):
        return lax.ppermute(x, everyone, [(i, i ^ masks[i & 1]) for i in range(devices)])

    grads = [
        lax.ppermute(back[k - 1], "group", [(i, i ^ k) for i in range(peers)])
        for k in range(1, peers)
    ]
    total = keep + swap(send, (1, 1))
    bits = devices.bit_length() - 1
    masks = [1 << b for b in range(1, bits)][::-1]
    masks = [masks[1], masks[0] | masks[1]] + masks[2:]
    for s in range(len(masks)):
        other = s ^ 1 if (s ^ 1) < len(masks) else s
        total = total + swap(total, (masks[s], masks[other]))
    partner = swap(total, (1, 1))
    weight_grad, loss = call(
        functools.partial(finish_kernel, row_count, row_count * devices),
        (sds((2 * width, width), f32), sds((1, 1), f32)),
        (total, partner),
        [VMEM, VMEM],
        (VMEM, SMEM),
        name="finish",
    )

    me = lax.axis_index("group")
    asked = jnp.stack(
        [
            lax.dynamic_slice_in_dim(pieces[k][bound_count], me, 1)[0, :capacity]
            for k in range(1, peers)
        ]
    ).astype(jnp.int32)
    feature_grad = call(
        return_kernel,
        sds((block_count, BLK, width), f32),
        (boundary, asked, own) + tuple(grads),
        [SMEM, SMEM] + [VMEM] * peers,
        VMEM,
        name="return",
    )
    return feature_grad.reshape(row_count, width), weight_grad, loss.reshape(())


def solution(mesh):
    return jax.shard_map(
        per_device,
        mesh=mesh,
        in_specs=(
            P(("dom", "group"), None),
            P(("dom", "group")),
            P(("dom", "group"), None),
            P(("dom", "group"), None),
            P(("dom", "group"), None),
            P(("dom", "group"), None),
            P(),
        ),
        out_specs=(P(("dom", "group"), None), P(), P()),
        check_vma=False,
    )
```

time: 265 us -> 104 us (0.39)
  other arithmetic: 66.5 us -> 1.68 us
  waiting for transfers between devices: 104 us -> 51.4 us
  blocking collectives: 39.4 us -> 0 us
  Pallas kernels: 0 us -> 31.6 us
  local copies, waits for them, and re-layouts: 24 us -> 3.2 us
  between operations: 16.5 us -> 0.79 us
  starting transfers between devices: 0.3 us -> 14.9 us
  matrix products: 12.6 us -> 0 us
    ppermute x0 -> x12, waiting for transfers between devices: none -> 51.4 us  [the longest x6 25.3 us: swap(): lax.ppermute(x, everyone, [(i, i ^ masks[i & 1]) for i in range(devices)])]
    reduce_scatter x1 -> x0, waiting for transfers between devices: 44.3 us -> none  [per_device(): lax.psum_scatter(sectioned.reshape(peer_count * bound_count * BLK, featur...]
    psum x1 -> x0, waiting for transfers between devices: 41.4 us -> none  [per_device(): totals = lax.psum((dweight, loss_sum), ('dom', 'group'))]
    scatter-add x3 -> x0, other arithmetic: 40.4 us -> none  [the longest x1 17.5 us: per_device(): table_grad.at[slot_list].add(dcandidates.reshape(-1, BLK, feature_width))]
    psum x1 -> x0, blocking collectives: 39.4 us -> none  [per_device(): totals = lax.psum((dweight, loss_sum), ('dom', 'group'))]
    pallas_call x0 -> x5, Pallas kernels: none -> 31.6 us  [call(): pl.pallas_call(kernel, out_shape=out_shape, in_specs=specs, out_specs=out...]
    all_gather x1 -> x0, waiting for transfers between devices: 18.7 us -> none  [per_device(): lax.all_gather(shared, 'group', axis=0, tiled=True)]
    ppermute x0 -> x12, starting transfers between devices: none -> 14.9 us  [the longest x6 10.1 us: swap(): lax.ppermute(x, everyone, [(i, i ^ masks[i & 1]) for i in range(devices)])]
  transfers between devices with their start and end apart: 3 -> 12, of which waited for: 3 -> 8; matrix products, arithmetic and copies ran while one was open for 21% -> 1% of each run, Pallas kernels for 0% -> 9%
where the time goes in v1:
time: 104 us
  waiting for transfers between devices  51.4 us (49%)
  Pallas kernels  31.6 us (30%)
  starting transfers between devices  14.9 us (14%)
  local copies, waits for them, and re-layouts  3.2 us (3%)
  other arithmetic  1.68 us (2%)
    pallas_call x5, Pallas kernels, call(): pl.pallas_call(kernel, out_shape=out_shape, in_specs=specs, out_specs=out...  31.6 us
    ppermute x6, waiting for transfers between devices, swap(): lax.ppermute(x, everyone, [(i, i ^ masks[i & 1]) for i in range(devices)])  25.3 us
    ppermute x3, waiting for transfers between devices, per_device(): lax.ppermute(back[k - 1], 'group', [(i, i ^ k) for i in range(peers)])  13.8 us
    ppermute x3, waiting for transfers between devices, per_device(): pieces[k | bit] = lax.ppermute(pieces[k], 'group', pairs)  12.3 us
    ppermute x6, starting transfers between devices, swap(): lax.ppermute(x, everyone, [(i, i ^ masks[i & 1]) for i in range(devices)])  10.1 us
    ppermute x3, starting transfers between devices, per_device(): pieces[k | bit] = lax.ppermute(pieces[k], 'group', pairs)  3 us
    unnamed x22, local copies, waits for them, and re-layouts  2.45 us
  transfers between devices with their start and end apart: 12, of which 8 were waited for; matrix products, arithmetic and copies ran while one was open for 1% of the time, Pallas kernels for 9%

profile of v1, /device:TPU:0, one launch (start us, length us, event | category | flops | bytes accessed | tf_op | source)
XLA Modules:
  0.0 103.6 jit_solution(11019176922277018483)
XLA Ops:
  0.6 2.3 %share.1 = bf16[65,16,256]{2,1,0:T(8,128)(2,1)} custom-call(s32[64]{0:T(128)} %boundary.5, s32[4,24]{1,0:T(4,128)} %request.3, bf16[128,16,256]{2,1,0:T(8,128)(2,1)} %bitcast.13), custom_call_target="tpu_custom_call" | custom-call | bytes 1049216 | tf_op jit(solution)/shard_map/share/pallas_call | solution.py:31
  2.9 3.0 %collective-permute-start.1 = (bf16[65,16,256]{2,1,0:T(8,128)(2,1)}, bf16[65,16,256]{2,1,0:T(8,128)(2,1)S(1)}, u32[]{:S(2)}, u32[]{:S(2)}) collective-permute-start(bf16[65,16,256]{2,1,0:T(8,128)(2,1)} %share.1), channel_id=1, source_target_pairs={{0,2},{1,3},{2,0},{3,1},{4,6},{5,7},{6,4},{7,5},{8,10},{9,11},{10,... | collective-permute-start | bytes 1597448 | tf_op jit(solution)/shard_map/ppermute | solution.py:273
  5.9 12.3 %collective-permute-done.1.rest_1_ = bf16[65,16,256]{2,1,0:T(8,128)(2,1)S(1)} collective-permute-done((bf16[65,16,256]{2,1,0:T(8,128)(2,1)}, bf16[65,16,256]{2,1,0:T(8,128)(2,1)S(1)}, u32[]{:S(2)}, u32[]{:S(2)}) %collective-permute-start.1) | collective-permute-done | bytes 532512 | tf_op jit(solution)/shard_map/ppermute | solution.py:273
  18.2 5.1 %early.1 = (bf16[2048,128]{1,0:T(8,128)(2,1)}, f32[2048,256]{1,0:T(8,128)}) custom-call(bf16[2048,256]{1,0:T(8,128)(2,1)} %feat.3, bf16[512,256]{1,0:T(8,128)(2,1)} %weight.3, s32[10,2048]{1,0:T(8,128)} %bitcast.15), custom_call_target="tpu_custom_call" | custom-call | flops 2147483648 | bytes 1392640 | tf_op jit(solution)/shard_map/early/pallas_call | solution.py:31
  23.3 0.0 collective-permute-done.rest_0_
  23.3 0.0 collective-permute-done.2.rest_2_
  23.3 0.8 copy-done.5
  24.1 0.2 copy-done.6
  24.3 18.6 %main.1 = (f32[128,16,256]{2,1,0:T(8,128)}, f32[264,256]{1,0:T(8,128)}, f32[264,256]{1,0:T(8,128)}, f32[24,16,256]{2,1,0:T(8,128)}, f32[24,16,256]{2,1,0:T(8,128)}, /*index=5*/f32[24,16,256]{2,1,0:T(8,128)}) custom-call(s32[8,16]{1,0:T(8,128)} %bitcast.18, s32[4,24]{1,0:T(4,128)} %request.3, s32[64]{0:T(128)} %boundary.5, bf16[128,16,256]{2,1,0:T(8,128)(2,1)} %bitcast.14, ...), custom_call_target="tpu_custom_call" | custom-call | flops 5368709120 | bytes 6694016 | tf_op jit(solution)/shard_map/main/pallas_call | solution.py:31
  42.9 0.4 collective-permute-start.6
  43.3 1.4 %collective-permute-done.6 = f32[264,256]{1,0:T(8,128)S(1)} collective-permute-done((f32[264,256]{1,0:T(8,128)}, f32[264,256]{1,0:T(8,128)S(1)}, u32[]{:S(2)}, u32[]{:S(2)}) %collective-permute-start.6) | collective-permute-done | bytes 270368 | tf_op jit(solution)/shard_map/ppermute | solution.py:316
  44.8 1.0 add.21
  45.8 1.9 %collective-permute-start.7 = (f32[264,256]{1,0:T(8,128)S(1)}, f32[264,256]{1,0:T(8,128)S(1)}, u32[]{:S(2)}, u32[]{:S(2)}) collective-permute-start(f32[264,256]{1,0:T(8,128)S(1)} %add.21), channel_id=1, source_target_pairs={{0,8},{1,25},{2,10},{3,27},{4,12},{5,29},{6,14},{7,31},{8,0},{9,17... | collective-permute-start | bytes 811016 | tf_op jit(solution)/shard_map/ppermute | solution.py:316
  47.6 6.9 %collective-permute-done.7 = f32[264,256]{1,0:T(8,128)S(1)} collective-permute-done((f32[264,256]{1,0:T(8,128)S(1)}, f32[264,256]{1,0:T(8,128)S(1)}, u32[]{:S(2)}, u32[]{:S(2)}) %collective-permute-start.7) | collective-permute-done | bytes 270368 | tf_op jit(solution)/shard_map/ppermute | solution.py:316
  54.6 4.5 %collective-permute-start.8 = (f32[264,256]{1,0:T(8,128)S(1)}, f32[264,256]{1,0:T(8,128)S(1)}, u32[]{:S(2)}, u32[]{:S(2)}) collective-permute-start(f32[264,256]{1,0:T(8,128)S(1)} %add.22), channel_id=1, source_target_pairs={{0,24},{1,9},{2,26},{3,11},{4,28},{5,13},{6,30},{7,15},{8,16},{9,1... | collective-permute-start | bytes 811016 | tf_op jit(solution)/shard_map/ppermute | solution.py:316
  59.1 6.2 %collective-permute-done.8 = f32[264,256]{1,0:T(8,128)S(1)} collective-permute-done((f32[264,256]{1,0:T(8,128)S(1)}, f32[264,256]{1,0:T(8,128)S(1)}, u32[]{:S(2)}, u32[]{:S(2)}) %collective-permute-start.8) | collective-permute-done | bytes 270368 | tf_op jit(solution)/shard_map/ppermute | solution.py:316
  65.4 1.5 %collective-permute-start.9 = (f32[264,256]{1,0:T(8,128)S(1)}, f32[264,256]{1,0:T(8,128)S(1)}, u32[]{:S(2)}, u32[]{:S(2)}) collective-permute-start(f32[264,256]{1,0:T(8,128)S(1)} %add.23), channel_id=1, source_target_pairs={{0,4},{1,3},{2,6},{3,1},{4,0},{5,7},{6,2},{7,5},{8,12},{9,11},{10,... | collective-permute-start | bytes 811016 | tf_op jit(solution)/shard_map/ppermute | solution.py:316
  66.9 7.0 %collective-permute-done.9 = f32[264,256]{1,0:T(8,128)S(1)} collective-permute-done((f32[264,256]{1,0:T(8,128)S(1)}, f32[264,256]{1,0:T(8,128)S(1)}, u32[]{:S(2)}, u32[]{:S(2)}) %collective-permute-start.9) | collective-permute-done | bytes 270368 | tf_op jit(solution)/shard_map/ppermute | solution.py:316
  73.9 1.7 %collective-permute-start.10 = (f32[264,256]{1,0:T(8,128)S(1)}, f32[264,256]{1,0:T(8,128)S(1)}, u32[]{:S(2)}, u32[]{:S(2)}) collective-permute-start(f32[264,256]{1,0:T(8,128)S(1)} %add.24), channel_id=1, source_target_pairs={{0,2},{1,5},{2,0},{3,7},{4,6},{5,1},{6,4},{7,3},{8,10},{9,13},{10,... | collective-permute-start | bytes 811016 | tf_op jit(solution)/shard_map/ppermute | solution.py:316
  75.6 0.7 slice.26
  76.3 0.0 collective-permute-start.3
  76.3 0.4 collective-permute-start.4
  76.8 1.4 %collective-permute-start.5 = (f32[24,16,256]{2,1,0:T(8,128)S(1)}, f32[24,16,256]{2,1,0:T(8,128)S(1)}, u32[]{:S(2)}, u32[]{:S(2)}) collective-permute-start(f32[24,16,256]{2,1,0:T(8,128)S(1)} %copy-done.8), channel_id=1, source_target_pairs={{0,3},{1,2},{2,1},{3,0},{4,7},{5,6},{6,5},{7,4},{8,11},{9,10},{10,... | collective-permute-start | bytes 1179656 | tf_op jit(solution)/shard_map/ppermute | solution.py:319
  78.2 3.7 %collective-permute-done.10 = f32[264,256]{1,0:T(8,128)S(1)} collective-permute-done((f32[264,256]{1,0:T(8,128)S(1)}, f32[264,256]{1,0:T(8,128)S(1)}, u32[]{:S(2)}, u32[]{:S(2)}) %collective-permute-start.10) | collective-permute-done | bytes 270368 | tf_op jit(solution)/shard_map/ppermute | solution.py:316
  81.9 0.1 collective-permute-start.11
  82.1 0.6 maximum_convert_fusion.asked
  82.7 7.6 %collective-permute-done.4.rest_1_ = f32[24,16,256]{2,1,0:T(8,128)S(1)} collective-permute-done((f32[24,16,256]{2,1,0:T(8,128)S(1)}, f32[24,16,256]{2,1,0:T(8,128)S(1)}, u32[]{:S(2)}, u32[]{:S(2)}) %collective-permute-start.4) | collective-permute-done | bytes 393248 | tf_op jit(solution)/shard_map/ppermute | solution.py:319
  90.3 6.2 %collective-permute-done.5.rest_2_ = f32[24,16,256]{2,1,0:T(8,128)S(1)} collective-permute-done((f32[24,16,256]{2,1,0:T(8,128)S(1)}, f32[24,16,256]{2,1,0:T(8,128)S(1)}, u32[]{:S(2)}, u32[]{:S(2)}) %collective-permute-start.5) | collective-permute-done | bytes 393248 | tf_op jit(solution)/shard_map/ppermute | solution.py:319
  96.5 0.8 copy-done.3
  97.2 3.7 %return.1 = f32[128,16,256]{2,1,0:T(8,128)} custom-call(s32[64]{0:T(128)} %boundary.5, s32[3,24]{1,0:T(4,128)} %maximum_convert_fusion.asked, f32[128,16,256]{2,1,0:T(8,128)} %get-tuple-element.15.own_in, f32[24,16,256]{2,1,0:T(8,128)} %copy-done.1, f32[24,16,256]{2,1,0:T(8,128)} %copy-done.2, f32[24,16,256]{2,1,0:T(8,128)} %copy-done.3), custom_call_target="tpu_custom_call" | custom-call | bytes 3277344 | tf_op jit(solution)/shard_map/return/pallas_call | solution.py:31
  101.0 0.7 copy-done.4
  101.7 1.9 %finish.1 = (f32[512,256]{1,0:T(8,128)}, f32[1,1]{1,0:T(1,128)}) custom-call(f32[264,256]{1,0:T(8,128)} %copy-done, f32[264,256]{1,0:T(8,128)} %copy-done.4), custom_call_target="tpu_custom_call" | custom-call | bytes 540672 | tf_op jit(solution)/shard_map/finish/pallas_call | solution.py:31
  (36 shorter events, 0.2 us)
Async XLA Ops:
  2.9 15.3 %collective-permute-start.1 = (bf16[65,16,256]{2,1,0:T(8,128)(2,1)}, bf16[65,16,256]{2,1,0:T(8,128)(2,1)S(1)}, u32[]{:S(2)}, u32[]{:S(2)}) collective-permute-start(bf16[65,16,256]{2,1,0:T(8,128)(2,1)} %share.1), channel_id=1, source_target_pairs={{0,2},{1,3},{2,0},{3,1},{4,6},{5,7},{6,4},{7,5},{8,10},{9,11},{10,... | collective-permute-start | bytes 1597448 | tf_op jit(solution)/shard_map/ppermute | solution.py:273
  5.9 17.4 %collective-permute-start = (bf16[65,16,256]{2,1,0:T(8,128)(2,1)}, bf16[65,16,256]{2,1,0:T(8,128)(2,1)S(1)}, u32[]{:S(2)}, u32[]{:S(2)}) collective-permute-start(bf16[65,16,256]{2,1,0:T(8,128)(2,1)} %share.1), channel_id=1, source_target_pairs={{0,1},{1,0},{2,3},{3,2},{4,5},{5,4},{6,7},{7,6},{8,9},{9,8},{10,11... | collective-permute-start | bytes 1597448 | tf_op jit(solution)/shard_map/ppermute | solution.py:273
  18.2 5.1 %copy-start.7 = (bf16[65,16,256]{2,1,0:T(8,128)(2,1)}, bf16[65,16,256]{2,1,0:T(8,128)(2,1)S(1)}, u32[]{:S(2)}) copy-start(bf16[65,16,256]{2,1,0:T(8,128)(2,1)S(1)} %collective-permute-done.1.rest_1_) | copy-start | bytes 1597444
  18.2 5.1 %collective-permute-start.2 = (bf16[65,16,256]{2,1,0:T(8,128)(2,1)S(1)}, bf16[65,16,256]{2,1,0:T(8,128)(2,1)S(1)}, u32[]{:S(2)}, u32[]{:S(2)}) collective-permute-start(bf16[65,16,256]{2,1,0:T(8,128)(2,1)S(1)} %collective-permute-done.1.rest_1_), channel_id=1, source_target_pairs={{0,1},{1,0},{2,3},{3,2},{4,5},{5,4},{6,7},{7,6},{8,9},{9,8},{10,11... | collective-permute-start | bytes 1597448 | tf_op jit(solution)/shard_map/ppermute | solution.py:273
  23.3 0.8 copy-start.5
  23.3 1.0 copy-start.6
  42.9 33.4 %copy-start.10 = (f32[24,16,256]{2,1,0:T(8,128)S(1)}, f32[24,16,256]{2,1,0:T(8,128)}, u32[]{:S(2)}) copy-start(f32[24,16,256]{2,1,0:T(8,128)} %get-tuple-element.16) | copy-start | bytes 1179652
  42.9 33.4 %copy-start.9 = (f32[24,16,256]{2,1,0:T(8,128)S(1)}, f32[24,16,256]{2,1,0:T(8,128)}, u32[]{:S(2)}) copy-start(f32[24,16,256]{2,1,0:T(8,128)} %get-tuple-element.17) | copy-start | bytes 1179652
  42.9 33.9 %copy-start.8 = (f32[24,16,256]{2,1,0:T(8,128)S(1)}, f32[24,16,256]{2,1,0:T(8,128)}, u32[]{:S(2)}) copy-start(f32[24,16,256]{2,1,0:T(8,128)} %get-tuple-element.18) | copy-start | bytes 1179652
  42.9 39.1 %slice-start = ((bf16[65,16,256]{2,1,0:T(8,128)(2,1)}), bf16[1,16,256]{2,1,0:T(8,128)(2,1)S(1)}, s32[]{:S(2)}) async-start(bf16[65,16,256]{2,1,0:T(8,128)(2,1)} %copy-done.5), calls=%async_computation | async-start | bytes 16384 | tf_op jit(solution)/shard_map/slice | solution.py:342
  42.9 39.1 %slice-start.1 = ((bf16[65,16,256]{2,1,0:T(8,128)(2,1)}), bf16[1,16,256]{2,1,0:T(8,128)(2,1)S(1)}, s32[]{:S(2)}) async-start(bf16[65,16,256]{2,1,0:T(8,128)(2,1)} %copy-done.6), calls=%async_computation.1 | async-start | bytes 16384 | tf_op jit(solution)/shard_map/slice | solution.py:342
  42.9 1.8 %collective-permute-start.6 = (f32[264,256]{1,0:T(8,128)}, f32[264,256]{1,0:T(8,128)S(1)}, u32[]{:S(2)}, u32[]{:S(2)}) collective-permute-start(f32[264,256]{1,0:T(8,128)} %get-tuple-element.20), channel_id=1, source_target_pairs={{0,1},{1,0},{2,3},{3,2},{4,5},{5,4},{6,7},{7,6},{8,9},{9,8},{10,11... | collective-permute-start | bytes 811016 | tf_op jit(solution)/shard_map/ppermute | solution.py:316
  45.8 8.8 %collective-permute-start.7 = (f32[264,256]{1,0:T(8,128)S(1)}, f32[264,256]{1,0:T(8,128)S(1)}, u32[]{:S(2)}, u32[]{:S(2)}) collective-permute-start(f32[264,256]{1,0:T(8,128)S(1)} %add.21), channel_id=1, source_target_pairs={{0,8},{1,25},{2,10},{3,27},{4,12},{5,29},{6,14},{7,31},{8,0},{9,17... | collective-permute-start | bytes 811016 | tf_op jit(solution)/shard_map/ppermute | solution.py:316
  54.6 10.8 %collective-permute-start.8 = (f32[264,256]{1,0:T(8,128)S(1)}, f32[264,256]{1,0:T(8,128)S(1)}, u32[]{:S(2)}, u32[]{:S(2)}) collective-permute-start(f32[264,256]{1,0:T(8,128)S(1)} %add.22), channel_id=1, source_target_pairs={{0,24},{1,9},{2,26},{3,11},{4,28},{5,13},{6,30},{7,15},{8,16},{9,1... | collective-permute-start | bytes 811016 | tf_op jit(solution)/shard_map/ppermute | solution.py:316
  65.4 8.5 %collective-permute-start.9 = (f32[264,256]{1,0:T(8,128)S(1)}, f32[264,256]{1,0:T(8,128)S(1)}, u32[]{:S(2)}, u32[]{:S(2)}) collective-permute-start(f32[264,256]{1,0:T(8,128)S(1)} %add.23), channel_id=1, source_target_pairs={{0,4},{1,3},{2,6},{3,1},{4,0},{5,7},{6,2},{7,5},{8,12},{9,11},{10,... | collective-permute-start | bytes 811016 | tf_op jit(solution)/shard_map/ppermute | solution.py:316
  73.9 8.0 %collective-permute-start.10 = (f32[264,256]{1,0:T(8,128)S(1)}, f32[264,256]{1,0:T(8,128)S(1)}, u32[]{:S(2)}, u32[]{:S(2)}) collective-permute-start(f32[264,256]{1,0:T(8,128)S(1)} %add.24), channel_id=1, source_target_pairs={{0,2},{1,5},{2,0},{3,7},{4,6},{5,1},{6,4},{7,3},{8,10},{9,13},{10,... | collective-permute-start | bytes 811016 | tf_op jit(solution)/shard_map/ppermute | solution.py:316
  76.3 6.3 %collective-permute-start.3 = (f32[24,16,256]{2,1,0:T(8,128)S(1)}, f32[24,16,256]{2,1,0:T(8,128)S(1)}, u32[]{:S(2)}, u32[]{:S(2)}) collective-permute-start(f32[24,16,256]{2,1,0:T(8,128)S(1)} %copy-done.10), channel_id=1, source_target_pairs={{0,1},{1,0},{2,3},{3,2},{4,5},{5,4},{6,7},{7,6},{8,9},{9,8},{10,11... | collective-permute-start | bytes 1179656 | tf_op jit(solution)/shard_map/ppermute | solution.py:319
  76.3 14.0 %collective-permute-start.4 = (f32[24,16,256]{2,1,0:T(8,128)S(1)}, f32[24,16,256]{2,1,0:T(8,128)S(1)}, u32[]{:S(2)}, u32[]{:S(2)}) collective-permute-start(f32[24,16,256]{2,1,0:T(8,128)S(1)} %copy-done.9), channel_id=1, source_target_pairs={{0,2},{1,3},{2,0},{3,1},{4,6},{5,7},{6,4},{7,5},{8,10},{9,11},{10,... | collective-permute-start | bytes 1179656 | tf_op jit(solution)/shard_map/ppermute | solution.py:319
  76.8 19.7 %collective-permute-start.5 = (f32[24,16,256]{2,1,0:T(8,128)S(1)}, f32[24,16,256]{2,1,0:T(8,128)S(1)}, u32[]{:S(2)}, u32[]{:S(2)}) collective-permute-start(f32[24,16,256]{2,1,0:T(8,128)S(1)} %copy-done.8), channel_id=1, source_target_pairs={{0,3},{1,2},{2,1},{3,0},{4,7},{5,6},{6,5},{7,4},{8,11},{9,10},{10,... | collective-permute-start | bytes 1179656 | tf_op jit(solution)/shard_map/ppermute | solution.py:319
  81.9 19.0 %copy-start = (f32[264,256]{1,0:T(8,128)}, f32[264,256]{1,0:T(8,128)S(1)}, u32[]{:S(2)}) copy-start(f32[264,256]{1,0:T(8,128)S(1)} %add.25.mine) | copy-start | bytes 811012
  81.9 19.0 %collective-permute-start.11 = (f32[264,256]{1,0:T(8,128)S(1)}, f32[264,256]{1,0:T(8,128)S(1)}, u32[]{:S(2)}, u32[]{:S(2)}) collective-permute-start(f32[264,256]{1,0:T(8,128)S(1)} %add.25.mine), channel_id=1, source_target_pairs={{0,1},{1,0},{2,3},{3,2},{4,5},{5,4},{6,7},{7,6},{8,9},{9,8},{10,11... | collective-permute-start | bytes 811016 | tf_op jit(solution)/shard_map/ppermute | solution.py:316
  82.7 13.8 %copy-start.1 = (f32[24,16,256]{2,1,0:T(8,128)}, f32[24,16,256]{2,1,0:T(8,128)S(1)}, u32[]{:S(2)}) copy-start(f32[24,16,256]{2,1,0:T(8,128)S(1)} %collective-permute-done.3.rest_0_) | copy-start | bytes 1179652
  90.3 6.2 %copy-start.2 = (f32[24,16,256]{2,1,0:T(8,128)}, f32[24,16,256]{2,1,0:T(8,128)S(1)}, u32[]{:S(2)}) copy-start(f32[24,16,256]{2,1,0:T(8,128)S(1)} %collective-permute-done.4.rest_1_) | copy-start | bytes 1179652
  96.5 0.8 copy-start.3
  101.0 0.7 copy-start.4

commit v2 on v1

--- a/solution.py
+++ b/solution.py
@@ -7,12 +7,14 @@
 from jax.experimental.pallas import tpu as pltpu
 from jax.sharding import PartitionSpec as P
 
+
 TILE = 128
 BLK = 16
 NBT = 8
 PAD = 8
 CHUNK = 4
 
+
 margin = 0.5
 epsilon = 1e-06
 
@@ -26,7 +28,7 @@
     return lax.dot_general(left, right, (dims, ((), ())), preferred_element_type=f32)
 
 
-def call(kernel, out_shape, args, specs, out_specs, scratch=(), flops=0, name=None):
+def call(kernel, out_shape, args, specs, out_specs, scratch=(), flops=0, limit=8):
     size = sum(a.size * a.dtype.itemsize for a in args)
     return pl.pallas_call(
         kernel,
@@ -35,7 +37,7 @@
         out_specs=out_specs,
         scratch_shapes=list(scratch),
         cost_estimate=pl.CostEstimate(flops=flops, bytes_accessed=size, transcendentals=0),
-        name=name,
+        compiler_params=pltpu.CompilerParams(vmem_limit_bytes=limit << 20),
     )(*args)
 
 
@@ -58,8 +60,27 @@
     out[count, :, 0:128] = tag.astype(bf16)
 
 
-def early_kernel(feat, weight, nbr, counts, pre):
+def early_kernel(slots, request, boundary, feat, weight, nbr, counts, pre, where_own, where_slot):
     rows, width = feat.shape
+    blocks = where_own.shape[0]
+    capacity = request.shape[1]
+    me = lax.axis_index("group")
+
+    def place(i, carry):
+        t = i // NBT
+        s = slots[i - t * NBT, t]
+        local = s < blocks
+        r = jnp.maximum(s - blocks, 0)
+        e = r // capacity
+        at = request[e, r - e * capacity]
+        mine = local | (e == me)
+        own_at = jnp.where(local, s, boundary[at])
+        where_own[i] = jnp.where(mine, own_at, -1)
+        spare = where_slot.shape[0] - 1
+        where_slot[jnp.where(local, spare, r)] = i
+        return carry
+
+    lax.fori_loop(0, blocks, place, 0, unroll=4)
     degree = nbr.shape[0]
     cand_ids = lax.broadcasted_iota(jnp.int32, (TILE, TILE), 0)
     top = weight[0:width, :]
@@ -84,41 +105,31 @@
     lax.fori_loop(0, rows // step, dense, 0)
 
 
-def main_kernel(peers, slots, request, boundary, feat3, feat, weight, nbr, neg, pre, counts, *rest):
+def main_kernel(peers, request, where_own, where_slot, feat, weight, nbr, neg, pre, counts, *rest):
     pieces = rest[: peers - 1]
     own, keep, send = rest[peers - 1 : peers + 2]
     back = rest[peers + 2 : 2 * peers + 1]
-    cand, agg, dpre, dcand, where_own, where_slot, wgrad, losses = rest[2 * peers + 1 :]
-    rows, width = feat.shape
-    blocks = feat3.shape[0]
+    cand, agg, dpre, dcand, wgrad, losses = rest[2 * peers + 1 :]
+    blocks, _, width = feat.shape
+    rows = blocks * BLK
     capacity = request.shape[1]
     degree = nbr.shape[0]
     negs = neg.shape[0]
     me = lax.axis_index("group")
 
-    def gather(i, carry):
-        t = i // NBT
-        s = slots[i - t * NBT, t]
-        local = s < blocks
-        r = jnp.maximum(s - blocks, 0)
-        e = r // capacity
-        at = request[e, r - e * capacity]
-        k = e ^ me
-        mine = local | (k == 0)
-        own_at = jnp.where(local, jnp.minimum(s, blocks - 1), boundary[at])
-        where_own[i] = jnp.where(mine, own_at, -1)
-
-        @pl.when(jnp.logical_not(local))
-        def _():
-            where_slot[r] = i
-
-        value = feat3[own_at]
-        for p in range(1, peers):
-            value = jnp.where(jnp.logical_not(mine) & (k == p), pieces[p - 1][at], value)
-        cand[i] = value
-        return carry
-
-    lax.fori_loop(0, blocks, gather, 0)
+    def fetch(i, carry):
+        cand[i] = feat[jnp.maximum(where_own[i], 0)]
+        return carry
+
+    lax.fori_loop(0, blocks, fetch, 0, unroll=8)
+    for k in range(1, peers):
+        peer = me ^ k
+
+        def fetch_far(c, carry, k=k, peer=peer):
+            cand[where_slot[peer * capacity + c]] = pieces[k - 1][request[peer, c]]
+            return carry
+
+        lax.fori_loop(0, capacity, fetch_far, 0, unroll=8)
     losses[...] = jnp.zeros(losses.shape, f32)
     top = weight[0:width, :]
     low = weight[width : 2 * width, :]
@@ -186,7 +197,7 @@
 
     lax.fori_loop(0, rows // step, chunk, 0)
 
-    wgrad[0:width, :] = dot(feat[...], dpre[...], ((0,), (0,)))
+    wgrad[0:width, :] = dot(feat[...].reshape(rows, width), dpre[...], ((0,), (0,)))
     wgrad[width : 2 * width, :] = dot(agg[...], dpre[...], ((0,), (0,)))
     half_rows = width
     core = me & 1
@@ -230,16 +241,30 @@
         lax.fori_loop(0, capacity, body, 0, unroll=4)
 
 
-def finish_kernel(rows, nodes, mine, other, wgrad, loss):
-    half_rows = mine.shape[0] - PAD
+def fold_kernel(masks, mine, other, keep, send):
+    quarter = keep.shape[0] - PAD
+    q = upper(masks, 0)
+    for out, at in ((keep, q), (send, 1 - q)):
+        rows = pl.ds(pl.multiple_of(at * quarter, quarter), quarter)
+        out[0:quarter, :] = mine[rows, :] + other[rows, :]
+        out[quarter:, :] = mine[2 * quarter :, :] + other[2 * quarter :, :]
+
+
+def upper(masks, flip):
+    i = lax.axis_index("dom") * lax.axis_size("group") + lax.axis_index("group")
+    core = (i & 1) ^ flip
+    return (i & jnp.where(core == 0, masks[0], masks[1]) != 0).astype(jnp.int32)
+
+
+def finish_kernel(masks, rows, nodes, mine, far, theirs, theirs_far, wgrad, loss):
+    quarter = mine.shape[0] - PAD
     core = lax.axis_index("group") & 1
-    wgrad[pl.ds(pl.multiple_of(core * half_rows, half_rows), half_rows), :] = (
-        mine[0:half_rows, :] / rows
-    )
-    wgrad[pl.ds(pl.multiple_of((1 - core) * half_rows, half_rows), half_rows), :] = (
-        other[0:half_rows, :] / rows
-    )
-    first = jnp.where(core == 0, mine[half_rows:, 0:128], other[half_rows:, 0:128])
+    for flip, pair in ((0, (mine, far)), (1, (theirs, theirs_far))):
+        q = upper(masks, flip)
+        for at, got in zip((q, 1 - q), pair):
+            to = ((core ^ flip) * 2 + at) * quarter
+            wgrad[pl.ds(pl.multiple_of(to, quarter), quarter), :] = got[0:quarter, :] / rows
+    first = jnp.where(core == 0, mine[quarter:, 0:128], theirs[quarter:, 0:128])
     loss[0, 0] = jnp.max(first) / nodes
 
 
@@ -263,7 +288,6 @@
         (boundary, request, blocks),
         [SMEM, SMEM, VMEM],
         VMEM,
-        name="share",
     )
     pieces = {0: shared}
     bit = peers // 2
@@ -273,14 +297,18 @@
             pieces[k | bit] = lax.ppermute(pieces[k], "group", pairs)
         bit //= 2
 
-    counts, pre = call(
+    counts, pre, where_own, where_slot = call(
         early_kernel,
-        (sds((row_count, TILE), bf16), sds((row_count, width), f32)),
-        (features, layer_weight, nbr),
-        [VMEM] * 3,
-        (VMEM, VMEM),
+        (
+            sds((row_count, TILE), bf16),
+            sds((row_count, width), f32),
+            sds((block_count,), jnp.int32),
+            sds((peers * capacity + 1,), jnp.int32),
+        ),
+        (slots, request, boundary, features, layer_weight, nbr),
+        [SMEM] * 3 + [VMEM] * 3,
+        (VMEM, VMEM, SMEM, SMEM),
         flops=2 * row_count * width * width * 8,
-        name="early",
     )
     outs = call(
         functools.partial(main_kernel, peers),
@@ -290,22 +318,20 @@
             sds((width + PAD, width), f32),
         )
         + (sds((capacity, BLK, width), f32),) * (peers - 1),
-        (slots, request, boundary, blocks, features, layer_weight, nbr, neg, pre, counts)
+        (request, where_own, where_slot, blocks, layer_weight, nbr, neg, pre, counts)
         + tuple(pieces[k] for k in range(1, peers)),
-        [SMEM] * 3 + [VMEM] * (6 + peers),
+        [SMEM] * 3 + [VMEM] * (5 + peers),
         (VMEM,) * (peers + 2),
         scratch=(
             pltpu.VMEM((block_count, BLK, width), bf16),
             pltpu.VMEM((row_count, width), bf16),
             pltpu.VMEM((row_count, width), bf16),
             pltpu.VMEM((block_count, BLK, width), f32),
-            pltpu.SMEM((block_count,), jnp.int32),
-            pltpu.SMEM((peers * capacity,), jnp.int32),
             pltpu.VMEM((2 * width, width), f32),
             pltpu.VMEM((8, TILE), f32),
         ),
         flops=2 * row_count * width * width * 20,
-        name="main",
+        limit=32,
     )
     own, keep, send = outs[:3]
     back = outs[3:]
@@ -319,21 +345,33 @@
         lax.ppermute(back[k - 1], "group", [(i, i ^ k) for i in range(peers)])
         for k in range(1, peers)
     ]
-    total = keep + swap(send, (1, 1))
-    bits = devices.bit_length() - 1
-    masks = [1 << b for b in range(1, bits)][::-1]
-    masks = [masks[1], masks[0] | masks[1]] + masks[2:]
-    for s in range(len(masks)):
-        other = s ^ 1 if (s ^ 1) < len(masks) else s
-        total = total + swap(total, (masks[s], masks[other]))
-    partner = swap(total, (1, 1))
+    bits = [1 << b for b in range(1, devices.bit_length() - 1)]
+    masks = bits[-2:] + [bits[-3], bits[0]] + bits[1:-3]
+    stages = []
+    for s in range(0, len(masks), 2):
+        pair = (masks[s], masks[min(s + 1, len(masks) - 1)])
+        stages += [pair, pair[::-1]][: len(masks) - s]
+    split = stages[0]
+    quarter = sds((width // 2 + PAD, width), f32)
+    total, send = call(
+        functools.partial(fold_kernel, split),
+        (quarter, quarter),
+        (keep, swap(send, (1, 1))),
+        [VMEM, VMEM],
+        (VMEM, VMEM),
+    )
+    total = total + swap(send, split)
+    for pair in stages[1:]:
+        total = total + swap(total, pair)
+    far = swap(total, split)
+    theirs = swap(total, (1, 1))
+    theirs_far = swap(far, (1, 1))
     weight_grad, loss = call(
-        functools.partial(finish_kernel, row_count, row_count * devices),
+        functools.partial(finish_kernel, split, row_count, row_count * devices),
         (sds((2 * width, width), f32), sds((1, 1), f32)),
-        (total, partner),
-        [VMEM, VMEM],
+        (total, far, theirs, theirs_far),
+        [VMEM] * 4,
         (VMEM, SMEM),
-        name="finish",
     )
 
     me = lax.axis_index("group")
@@ -349,7 +387,6 @@
         (boundary, asked, own) + tuple(grads),
         [SMEM, SMEM] + [VMEM] * peers,
         VMEM,
-        name="return",
     )
     return feature_grad.reshape(row_count, width), weight_grad, loss.reshape(())
 

time: 104 us -> 86 us (0.83)
  Pallas kernels: 31.6 us -> 20.1 us
  waiting for transfers between devices: 51.4 us -> 41.5 us
  local copies, waits for them, and re-layouts: 3.2 us -> 6.79 us
  other arithmetic: 1.68 us -> 0.1 us
  starting transfers between devices: 14.9 us -> 16.3 us
    pallas_call x5 -> x6, Pallas kernels: 31.6 us -> 20.1 us  [call(): pl.pallas_call(kernel, out_shape=out_shape, in_specs=specs, out_specs=out...]
    ppermute x6 -> x8, waiting for transfers between devices: 25.3 us -> 18.5 us  [swap(): lax.ppermute(x, everyone, [(i, i ^ masks[i & 1]) for i in range(devices)])]
    unnamed x22 -> x32, local copies, waits for them, and re-layouts: 2.45 us -> 6.04 us
    ppermute x3, waiting for transfers between devices: 13.8 us -> 10.9 us  [per_device(): lax.ppermute(back[k - 1], 'group', [(i, i ^ k) for i in range(peers)])]
    ppermute x6 -> x8, starting transfers between devices: 10.1 us -> 11.4 us  [swap(): lax.ppermute(x, everyone, [(i, i ^ masks[i & 1]) for i in range(devices)])]
  transfers between devices with their start and end apart: 12 -> 14, of which waited for: 8 -> 9; matrix products, arithmetic and copies ran while one was open for 1% -> 1% of each run, Pallas kernels for 9% -> 9%
where the time goes in v2:
time: 86 us; the launch traced here: 85.7 us
  waiting for transfers between devices  41.5 us (48%)
  Pallas kernels  20.1 us (23%)
  starting transfers between devices  16.3 us (19%)
  local copies, waits for them, and re-layouts  6.79 us (8%)
    pallas_call x6, Pallas kernels, call(): pl.pallas_call(kernel, out_shape=out_shape, in_specs=specs, out_specs=out...  20.1 us
    ppermute x8, waiting for transfers between devices, swap(): lax.ppermute(x, everyone, [(i, i ^ masks[i & 1]) for i in range(devices)])  18.5 us
    ppermute x3, waiting for transfers between devices, per_device(): pieces[k | bit] = lax.ppermute(pieces[k], 'group', pairs)  12.1 us
    ppermute x8, starting transfers between devices, swap(): lax.ppermute(x, everyone, [(i, i ^ masks[i & 1]) for i in range(devices)])  11.4 us
    ppermute x3, waiting for transfers between devices, per_device(): lax.ppermute(back[k - 1], 'group', [(i, i ^ k) for i in range(peers)])  10.9 us
    unnamed x32, local copies, waits for them, and re-layouts  6.04 us
    ppermute x3, starting transfers between devices, per_device(): pieces[k | bit] = lax.ppermute(pieces[k], 'group', pairs)  3.07 us
    ppermute x3, starting transfers between devices, per_device(): lax.ppermute(back[k - 1], 'group', [(i, i ^ k) for i in range(peers)])  1.86 us
  transfers between devices with their start and end apart: 14, of which 9 were waited for; matrix products, arithmetic and copies ran while one was open for 1% of the time, Pallas kernels for 9%

profile of v2, /device:TPU:0, one launch (start us, length us, event | category | flops | bytes accessed | tf_op | source)
XLA Modules:
  0.0 85.7 jit_solution(4791427062205148949)
XLA Ops:
  0.6 1.2 %copy-done = bf16[2048,256]{1,0:T(8,128)(2,1)S(1)} copy-done((bf16[2048,256]{1,0:T(8,128)(2,1)S(1)}, bf16[2048,256]{1,0:T(8,128)(2,1)}, u32[]{:S(2)}) %copy-start) | copy-done | bytes 1048600
  1.9 0.7 copy-done.2
  2.5 0.7 copy-done.4
  3.2 0.8 shard_map.94
  4.0 3.1 %collective-permute-start.1 = (bf16[65,16,256]{2,1,0:T(8,128)(2,1)S(1)}, bf16[65,16,256]{2,1,0:T(8,128)(2,1)S(1)}, u32[]{:S(2)}, u32[]{:S(2)}) collective-permute-start(bf16[65,16,256]{2,1,0:T(8,128)(2,1)S(1)} %shard_map.94), channel_id=1, source_target_pairs={{0,2},{1,3},{2,0},{3,1},{4,6},{5,7},{6,4},{7,5},{8,10},{9,11},{10,... | collective-permute-start | bytes 1597448 | tf_op jit(solution)/shard_map/ppermute | solution.py:297
  7.0 12.1 %collective-permute-done.1.rest_1_ = bf16[65,16,256]{2,1,0:T(8,128)(2,1)S(1)} collective-permute-done((bf16[65,16,256]{2,1,0:T(8,128)(2,1)S(1)}, bf16[65,16,256]{2,1,0:T(8,128)(2,1)S(1)}, u32[]{:S(2)}, u32[]{:S(2)}) %collective-permute-start.1) | collective-permute-done | bytes 532512 | tf_op jit(solution)/shard_map/ppermute | solution.py:297
  19.1 1.1 %copy-done.10 = bf16[512,256]{1,0:T(8,128)(2,1)S(1)} copy-done((bf16[512,256]{1,0:T(8,128)(2,1)S(1)}, bf16[512,256]{1,0:T(8,128)(2,1)}, u32[]{:S(2)}) %copy-start.10) | copy-done | bytes 262168
  20.3 0.9 %copy-done.12 = s32[2048,10]{0,1:T(8,128)S(1)} copy-done((s32[2048,10]{0,1:T(8,128)S(1)}, s32[2048,10]{0,1:T(8,128)}, u32[]{:S(2)}) %copy-start.12) | copy-done | bytes 81944
  21.2 0.7 copy-done.15
  21.9 5.7 %shard_map.95 = (bf16[2048,128]{1,0:T(8,128)(2,1)S(1)}, f32[2048,256]{1,0:T(8,128)S(1)}, s32[128]{0:T(128)S(1)}, s32[97]{0:T(128)S(1)}) custom-call(s32[8,16]{1,0:T(8,128)S(1)} %bitcast.17, s32[4,24]{1,0:T(4,128)S(1)} %copy-done.2, s32[64]{0:T(128)S(1)} %copy-done.4, bf16[2048,256]{1,0:T(8,128)(2,1)S(1)} %copy-done, bf16[512,256]{1,0:T(8,128)(2,1)S(1)} %copy-done.10, ...), custom_call_target="tpu_custom_call" | custom-call | flops 2147483648 | bytes 1393792 | tf_op jit(solution)/shard_map/pallas_call | solution.py:33
  27.6 10.3 %shard_map.96 = (f32[128,16,256]{2,1,0:T(8,128)S(1)}, f32[264,256]{1,0:T(8,128)S(1)}, f32[264,256]{1,0:T(8,128)S(1)}, f32[24,16,256]{2,1,0:T(8,128)S(1)}, f32[24...) custom-call(s32[4,24]{1,0:T(4,128)S(1)} %copy-done.3, s32[128]{0:T(128)S(1)} %get-tuple-element.17.where_own, ...), custom_call_target="tpu_custom_call" | custom-call | flops 5368709120 | bytes 5645572 | tf_op jit(solution)/shard_map/pallas_call | solution.py:33
  38.0 0.7 copy-done.9
  38.7 0.3 collective-permute-start.6
  39.1 1.2 %collective-permute-done.6.other = f32[264,256]{1,0:T(8,128)S(1)} collective-permute-done((f32[264,256]{1,0:T(8,128)S(1)}, f32[264,256]{1,0:T(8,128)S(1)}, u32[]{:S(2)}, u32[]{:S(2)}) %collective-permute-start.6) | collective-permute-done | bytes 270368 | tf_op jit(solution)/shard_map/ppermute | solution.py:342
  40.3 1.9 %collective-permute-start.7 = (f32[136,256]{1,0:T(8,128)S(1)}, f32[136,256]{1,0:T(8,128)S(1)}, u32[]{:S(2)}, u32[]{:S(2)}) collective-permute-start(f32[136,256]{1,0:T(8,128)S(1)} %get-tuple-element.28), channel_id=1, source_target_pairs={{0,8},{1,17},{2,10},{3,19},{4,12},{5,21},{6,14},{7,23},{8,0},{9,25... | collective-permute-start | bytes 417800 | tf_op jit(solution)/shard_map/ppermute | solution.py:342
  42.2 4.5 %collective-permute-done.7 = f32[136,256]{1,0:T(8,128)S(1)} collective-permute-done((f32[136,256]{1,0:T(8,128)S(1)}, f32[136,256]{1,0:T(8,128)S(1)}, u32[]{:S(2)}, u32[]{:S(2)}) %collective-permute-start.7) | collective-permute-done | bytes 139296 | tf_op jit(solution)/shard_map/ppermute | solution.py:342
  46.7 2.4 %collective-permute-start.8 = (f32[136,256]{1,0:T(8,128)S(1)}, f32[136,256]{1,0:T(8,128)S(1)}, u32[]{:S(2)}, u32[]{:S(2)}) collective-permute-start(f32[136,256]{1,0:T(8,128)S(1)} %add.18), channel_id=1, source_target_pairs={{0,16},{1,9},{2,18},{3,11},{4,20},{5,13},{6,22},{7,15},{8,24},{9,1... | collective-permute-start | bytes 417800 | tf_op jit(solution)/shard_map/ppermute | solution.py:342
  49.1 4.0 %collective-permute-done.8 = f32[136,256]{1,0:T(8,128)S(1)} collective-permute-done((f32[136,256]{1,0:T(8,128)S(1)}, f32[136,256]{1,0:T(8,128)S(1)}, u32[]{:S(2)}, u32[]{:S(2)}) %collective-permute-start.8) | collective-permute-done | bytes 139296 | tf_op jit(solution)/shard_map/ppermute | solution.py:342
  53.2 2.3 %collective-permute-start.9 = (f32[136,256]{1,0:T(8,128)S(1)}, f32[136,256]{1,0:T(8,128)S(1)}, u32[]{:S(2)}, u32[]{:S(2)}) collective-permute-start(f32[136,256]{1,0:T(8,128)S(1)} %add.19), channel_id=1, source_target_pairs={{0,4},{1,3},{2,6},{3,1},{4,0},{5,7},{6,2},{7,5},{8,12},{9,11},{10,... | collective-permute-start | bytes 417800 | tf_op jit(solution)/shard_map/ppermute | solution.py:342
  55.5 3.9 %collective-permute-done.9 = f32[136,256]{1,0:T(8,128)S(1)} collective-permute-done((f32[136,256]{1,0:T(8,128)S(1)}, f32[136,256]{1,0:T(8,128)S(1)}, u32[]{:S(2)}, u32[]{:S(2)}) %collective-permute-start.9) | collective-permute-done | bytes 139296 | tf_op jit(solution)/shard_map/ppermute | solution.py:342
  59.4 2.6 %collective-permute-start.10 = (f32[136,256]{1,0:T(8,128)S(1)}, f32[136,256]{1,0:T(8,128)S(1)}, u32[]{:S(2)}, u32[]{:S(2)}) collective-permute-start(f32[136,256]{1,0:T(8,128)S(1)} %add.20), channel_id=1, source_target_pairs={{0,2},{1,5},{2,0},{3,7},{4,6},{5,1},{6,4},{7,3},{8,10},{9,13},{10,... | collective-permute-start | bytes 417800 | tf_op jit(solution)/shard_map/ppermute | solution.py:342
  62.0 0.7 slice.26
  62.7 0.0 collective-permute-start.4
  62.7 1.8 %collective-permute-start.5 = (f32[24,16,256]{2,1,0:T(8,128)}, f32[24,16,256]{2,1,0:T(8,128)S(1)}, u32[]{:S(2)}, u32[]{:S(2)}) collective-permute-start(f32[24,16,256]{2,1,0:T(8,128)} %copy-done.7), channel_id=1, source_target_pairs={{0,3},{1,2},{2,1},{3,0},{4,7},{5,6},{6,5},{7,4},{8,11},{9,10},{10,... | collective-permute-start | bytes 1179656 | tf_op jit(solution)/shard_map/ppermute | solution.py:345
  64.5 0.8 collective-permute-done.10
  65.3 1.8 %collective-permute-start.11 = (f32[136,256]{1,0:T(8,128)S(1)}, f32[136,256]{1,0:T(8,128)S(1)}, u32[]{:S(2)}, u32[]{:S(2)}) collective-permute-start(f32[136,256]{1,0:T(8,128)S(1)} %add.21.mine), channel_id=1, source_target_pairs={{0,8},{1,17},{2,10},{3,19},{4,12},{5,21},{6,14},{7,23},{8,0},{9,25... | collective-permute-start | bytes 417800 | tf_op jit(solution)/shard_map/ppermute | solution.py:342
  67.2 0.1 collective-permute-start.12
  67.3 4.1 %collective-permute-done.11.far = f32[136,256]{1,0:T(8,128)S(1)} collective-permute-done((f32[136,256]{1,0:T(8,128)S(1)}, f32[136,256]{1,0:T(8,128)S(1)}, u32[]{:S(2)}, u32[]{:S(2)}) %collective-permute-start.11) | collective-permute-done | bytes 139296 | tf_op jit(solution)/shard_map/ppermute | solution.py:342
  71.4 3.4 %collective-permute-done.4.rest_1_ = f32[24,16,256]{2,1,0:T(8,128)S(1)} collective-permute-done((f32[24,16,256]{2,1,0:T(8,128)}, f32[24,16,256]{2,1,0:T(8,128)S(1)}, u32[]{:S(2)}, u32[]{:S(2)}) %collective-permute-start.4) | collective-permute-done | bytes 393248 | tf_op jit(solution)/shard_map/ppermute | solution.py:345
  74.9 7.5 %collective-permute-done.5.rest_2_ = f32[24,16,256]{2,1,0:T(8,128)S(1)} collective-permute-done((f32[24,16,256]{2,1,0:T(8,128)}, f32[24,16,256]{2,1,0:T(8,128)S(1)}, u32[]{:S(2)}, u32[]{:S(2)}) %collective-permute-start.5) | collective-permute-done | bytes 393248 | tf_op jit(solution)/shard_map/ppermute | solution.py:345
  82.4 2.4 %shard_map.97 = f32[128,16,256]{2,1,0:T(8,128)} custom-call(s32[64]{0:T(128)S(1)} %copy-done.5, s32[3,24]{1,0:T(4,128)S(1)} %maximum_convert_fusion.asked, f32[128,16,256]{2,1,0:T(8,128)S(1)} %get-tuple-element.21.own_in, f32[24,16,256]{2,1,0:T(8,128)S(1)} %collective-permute-done.3.rest_0_, f32[24,16,256]{2,1,0:T(8,128)S(1)} %collective-permute-done.4.rest_1_, ...), custom_call_target="tpu_custom_call" | custom-call | bytes 3277344 | tf_op jit(solution)/shard_map/pallas_call | solution.py:33
  84.8 0.9 %shard_map.99 = (f32[512,256]{1,0:T(8,128)}, f32[1,1]{1,0:T(1,128)}) custom-call(f32[136,256]{1,0:T(8,128)S(1)} %add.21.mine, f32[136,256]{1,0:T(8,128)S(1)} %collective-permute-done.11.far, f32[136,256]{1,0:T(8,128)S(1)} %collective-permute-done.12.theirs, f32[136,256]{1,0:T(8,128)S(1)} %collective-permute-done.13.theirs_far), custom_call_target="tpu_custom_call" | custom-call | bytes 557056 | tf_op jit(solution)/shard_map/pallas_call | solution.py:33
  (48 shorter events, 0.3 us)
Async XLA Ops:
  0.6 1.2 %copy-start = (bf16[2048,256]{1,0:T(8,128)(2,1)S(1)}, bf16[2048,256]{1,0:T(8,128)(2,1)}, u32[]{:S(2)}) copy-start(bf16[2048,256]{1,0:T(8,128)(2,1)} %feat.1) | copy-start | bytes 3145732
  1.9 0.7 copy-start.2
  2.5 0.7 copy-start.4
  4.0 15.2 %collective-permute-start.1 = (bf16[65,16,256]{2,1,0:T(8,128)(2,1)S(1)}, bf16[65,16,256]{2,1,0:T(8,128)(2,1)S(1)}, u32[]{:S(2)}, u32[]{:S(2)}) collective-permute-start(bf16[65,16,256]{2,1,0:T(8,128)(2,1)S(1)} %shard_map.94), channel_id=1, source_target_pairs={{0,2},{1,3},{2,0},{3,1},{4,6},{5,7},{6,4},{7,5},{8,10},{9,11},{10,... | collective-permute-start | bytes 1597448 | tf_op jit(solution)/shard_map/ppermute | solution.py:297
  7.0 20.5 %collective-permute-start = (bf16[65,16,256]{2,1,0:T(8,128)(2,1)S(1)}, bf16[65,16,256]{2,1,0:T(8,128)(2,1)S(1)}, u32[]{:S(2)}, u32[]{:S(2)}) collective-permute-start(bf16[65,16,256]{2,1,0:T(8,128)(2,1)S(1)} %shard_map.94), channel_id=1, source_target_pairs={{0,1},{1,0},{2,3},{3,2},{4,5},{5,4},{6,7},{7,6},{8,9},{9,8},{10,11... | collective-permute-start | bytes 1597448 | tf_op jit(solution)/shard_map/ppermute | solution.py:297
  19.1 8.4 %copy-start.6 = (bf16[65,16,256]{2,1,0:T(8,128)(2,1)}, bf16[65,16,256]{2,1,0:T(8,128)(2,1)S(1)}, u32[]{:S(2)}) copy-start(bf16[65,16,256]{2,1,0:T(8,128)(2,1)S(1)} %collective-permute-done.1.rest_1_) | copy-start | bytes 1597444
  19.1 8.4 %collective-permute-start.2 = (bf16[65,16,256]{2,1,0:T(8,128)(2,1)S(1)}, bf16[65,16,256]{2,1,0:T(8,128)(2,1)S(1)}, u32[]{:S(2)}, u32[]{:S(2)}) collective-permute-start(bf16[65,16,256]{2,1,0:T(8,128)(2,1)S(1)} %collective-permute-done.1.rest_1_), channel_id=1, source_target_pairs={{0,1},{1,0},{2,3},{3,2},{4,5},{5,4},{6,7},{7,6},{8,9},{9,8},{10,11... | collective-permute-start | bytes 1597448 | tf_op jit(solution)/shard_map/ppermute | solution.py:297
  19.1 1.1 %copy-start.10 = (bf16[512,256]{1,0:T(8,128)(2,1)S(1)}, bf16[512,256]{1,0:T(8,128)(2,1)}, u32[]{:S(2)}) copy-start(bf16[512,256]{1,0:T(8,128)(2,1)} %weight.3) | copy-start | bytes 786436
  20.3 0.9 %copy-start.12 = (s32[2048,10]{0,1:T(8,128)S(1)}, s32[2048,10]{0,1:T(8,128)}, u32[]{:S(2)}) copy-start(s32[2048,10]{0,1:T(8,128)} %param.11) | copy-start | bytes 245764
  21.2 0.7 copy-start.15
  21.9 5.7 %copy-start.1 = (bf16[2048,256]{1,0:T(8,128)(2,1)S(1)}, bf16[2048,256]{1,0:T(8,128)(2,1)}, u32[]{:S(2)}) copy-start(bf16[2048,256]{1,0:T(8,128)(2,1)} %feat.1) | copy-start | bytes 3145732
  21.9 5.8 %copy-start.3 = (s32[4,24]{1,0:T(4,128)S(1)}, s32[4,24]{1,0:T(4,128)}, u32[]{:S(2)}) copy-start(s32[4,24]{1,0:T(4,128)} %request.5) | copy-start | bytes 1156
  21.9 5.8 %copy-start.11 = (bf16[512,256]{1,0:T(8,128)(2,1)S(1)}, bf16[512,256]{1,0:T(8,128)(2,1)}, u32[]{:S(2)}) copy-start(bf16[512,256]{1,0:T(8,128)(2,1)} %weight.3) | copy-start | bytes 786436
  21.9 5.8 %copy-start.13 = (s32[2048,10]{0,1:T(8,128)S(1)}, s32[2048,10]{0,1:T(8,128)}, u32[]{:S(2)}) copy-start(s32[2048,10]{0,1:T(8,128)} %param.11) | copy-start | bytes 245764
  21.9 5.8 %copy-start.14 = (s32[2048,4]{0,1:T(4,128)S(1)}, s32[2048,4]{0,1:T(4,128)}, u32[]{:S(2)}) copy-start(s32[2048,4]{0,1:T(4,128)} %param.12) | copy-start | bytes 98308
  38.0 0.7 copy-start.9
  38.7 8.0 %copy-start.7 = (f32[24,16,256]{2,1,0:T(8,128)}, f32[24,16,256]{2,1,0:T(8,128)S(1)}, u32[]{:S(2)}) copy-start(f32[24,16,256]{2,1,0:T(8,128)S(1)} %get-tuple-element.24) | copy-start | bytes 1179652
  38.7 10.4 %copy-start.8 = (f32[24,16,256]{2,1,0:T(8,128)}, f32[24,16,256]{2,1,0:T(8,128)S(1)}, u32[]{:S(2)}) copy-start(f32[24,16,256]{2,1,0:T(8,128)S(1)} %get-tuple-element.23) | copy-start | bytes 1179652
  38.7 43.6 %copy-start.5 = (s32[64]{0:T(128)S(1)}, s32[64]{0:T(128)}, u32[]{:S(2)}) copy-start(s32[64]{0:T(128)} %boundary.5) | copy-start | bytes 772
  38.7 1.5 %collective-permute-start.6 = (f32[264,256]{1,0:T(8,128)S(1)}, f32[264,256]{1,0:T(8,128)S(1)}, u32[]{:S(2)}, u32[]{:S(2)}) collective-permute-start(f32[264,256]{1,0:T(8,128)S(1)} %get-tuple-element.26), channel_id=1, source_target_pairs={{0,1},{1,0},{2,3},{3,2},{4,5},{5,4},{6,7},{7,6},{8,9},{9,8},{10,11... | collective-permute-start | bytes 811016 | tf_op jit(solution)/shard_map/ppermute | solution.py:342
  40.3 6.4 %collective-permute-start.7 = (f32[136,256]{1,0:T(8,128)S(1)}, f32[136,256]{1,0:T(8,128)S(1)}, u32[]{:S(2)}, u32[]{:S(2)}) collective-permute-start(f32[136,256]{1,0:T(8,128)S(1)} %get-tuple-element.28), channel_id=1, source_target_pairs={{0,8},{1,17},{2,10},{3,19},{4,12},{5,21},{6,14},{7,23},{8,0},{9,25... | collective-permute-start | bytes 417800 | tf_op jit(solution)/shard_map/ppermute | solution.py:342
  46.7 6.4 %collective-permute-start.8 = (f32[136,256]{1,0:T(8,128)S(1)}, f32[136,256]{1,0:T(8,128)S(1)}, u32[]{:S(2)}, u32[]{:S(2)}) collective-permute-start(f32[136,256]{1,0:T(8,128)S(1)} %add.18), channel_id=1, source_target_pairs={{0,16},{1,9},{2,18},{3,11},{4,20},{5,13},{6,22},{7,15},{8,24},{9,1... | collective-permute-start | bytes 417800 | tf_op jit(solution)/shard_map/ppermute | solution.py:342
  53.2 6.2 %collective-permute-start.9 = (f32[136,256]{1,0:T(8,128)S(1)}, f32[136,256]{1,0:T(8,128)S(1)}, u32[]{:S(2)}, u32[]{:S(2)}) collective-permute-start(f32[136,256]{1,0:T(8,128)S(1)} %add.19), channel_id=1, source_target_pairs={{0,4},{1,3},{2,6},{3,1},{4,0},{5,7},{6,2},{7,5},{8,12},{9,11},{10,... | collective-permute-start | bytes 417800 | tf_op jit(solution)/shard_map/ppermute | solution.py:342
  59.4 5.9 %collective-permute-start.10 = (f32[136,256]{1,0:T(8,128)S(1)}, f32[136,256]{1,0:T(8,128)S(1)}, u32[]{:S(2)}, u32[]{:S(2)}) collective-permute-start(f32[136,256]{1,0:T(8,128)S(1)} %add.20), channel_id=1, source_target_pairs={{0,2},{1,5},{2,0},{3,7},{4,6},{5,1},{6,4},{7,3},{8,10},{9,13},{10,... | collective-permute-start | bytes 417800 | tf_op jit(solution)/shard_map/ppermute | solution.py:342
  62.7 8.8 %collective-permute-start.3 = (f32[24,16,256]{2,1,0:T(8,128)}, f32[24,16,256]{2,1,0:T(8,128)S(1)}, u32[]{:S(2)}, u32[]{:S(2)}) collective-permute-start(f32[24,16,256]{2,1,0:T(8,128)} %copy-done.9), channel_id=1, source_target_pairs={{0,1},{1,0},{2,3},{3,2},{4,5},{5,4},{6,7},{7,6},{8,9},{9,8},{10,11... | collective-permute-start | bytes 1179656 | tf_op jit(solution)/shard_map/ppermute | solution.py:345
  62.7 12.2 %collective-permute-start.4 = (f32[24,16,256]{2,1,0:T(8,128)}, f32[24,16,256]{2,1,0:T(8,128)S(1)}, u32[]{:S(2)}, u32[]{:S(2)}) collective-permute-start(f32[24,16,256]{2,1,0:T(8,128)} %copy-done.8), channel_id=1, source_target_pairs={{0,2},{1,3},{2,0},{3,1},{4,6},{5,7},{6,4},{7,5},{8,10},{9,11},{10,... | collective-permute-start | bytes 1179656 | tf_op jit(solution)/shard_map/ppermute | solution.py:345
  62.7 19.7 %collective-permute-start.5 = (f32[24,16,256]{2,1,0:T(8,128)}, f32[24,16,256]{2,1,0:T(8,128)S(1)}, u32[]{:S(2)}, u32[]{:S(2)}) collective-permute-start(f32[24,16,256]{2,1,0:T(8,128)} %copy-done.7), channel_id=1, source_target_pairs={{0,3},{1,2},{2,1},{3,0},{4,7},{5,6},{6,5},{7,4},{8,11},{9,10},{10,... | collective-permute-start | bytes 1179656 | tf_op jit(solution)/shard_map/ppermute | solution.py:345
  65.3 6.0 %collective-permute-start.11 = (f32[136,256]{1,0:T(8,128)S(1)}, f32[136,256]{1,0:T(8,128)S(1)}, u32[]{:S(2)}, u32[]{:S(2)}) collective-permute-start(f32[136,256]{1,0:T(8,128)S(1)} %add.21.mine), channel_id=1, source_target_pairs={{0,8},{1,17},{2,10},{3,19},{4,12},{5,21},{6,14},{7,23},{8,0},{9,25... | collective-permute-start | bytes 417800 | tf_op jit(solution)/shard_map/ppermute | solution.py:342
  67.2 17.6 %collective-permute-start.12 = (f32[136,256]{1,0:T(8,128)S(1)}, f32[136,256]{1,0:T(8,128)S(1)}, u32[]{:S(2)}, u32[]{:S(2)}) collective-permute-start(f32[136,256]{1,0:T(8,128)S(1)} %add.21.mine), channel_id=1, source_target_pairs={{0,1},{1,0},{2,3},{3,2},{4,5},{5,4},{6,7},{7,6},{8,9},{9,8},{10,11... | collective-permute-start | bytes 417800 | tf_op jit(solution)/shard_map/ppermute | solution.py:342
  71.4 13.4 %collective-permute-start.13 = (f32[136,256]{1,0:T(8,128)S(1)}, f32[136,256]{1,0:T(8,128)S(1)}, u32[]{:S(2)}, u32[]{:S(2)}) collective-permute-start(f32[136,256]{1,0:T(8,128)S(1)} %collective-permute-done.11.far), channel_id=1, source_target_pairs={{0,1},{1,0},{2,3},{3,2},{4,5},{5,4},{6,7},{7,6},{8,9},{9,8},{10,11... | collective-permute-start | bytes 417800 | tf_op jit(solution)/shard_map/ppermute | solution.py:342

commit v3 on v2

--- a/solution.py
+++ b/solution.py
@@ -107,9 +107,7 @@
 
 def main_kernel(peers, request, where_own, where_slot, feat, weight, nbr, neg, pre, counts, *rest):
     pieces = rest[: peers - 1]
-    own, keep, send = rest[peers - 1 : peers + 2]
-    back = rest[peers + 2 : 2 * peers + 1]
-    cand, agg, dpre, dcand, wgrad, losses = rest[2 * peers + 1 :]
+    keep, send, halves, dpre, dsc, cand, agg, wgrad, losses = rest[peers - 1 :]
     blocks, _, width = feat.shape
     rows = blocks * BLK
     capacity = request.shape[1]
@@ -131,7 +129,6 @@
 
         lax.fori_loop(0, capacity, fetch_far, 0, unroll=8)
     losses[...] = jnp.zeros(losses.shape, f32)
-    top = weight[0:width, :]
     low = weight[width : 2 * width, :]
     cand_ids = lax.broadcasted_iota(jnp.int32, (TILE, TILE), 0)
     step = CHUNK * TILE
@@ -153,8 +150,8 @@
         scale = lax.rsqrt(jnp.mean(hidden * hidden, axis=-1, keepdims=True) + epsilon)
         embedding = hidden * scale
         half = embedding.astype(bf16)
+        halves[at, :] = half
         demb = []
-        dsc = []
         for tt in range(CHUNK):
             t = c * CHUNK + tt
             lanes = pl.ds(pl.multiple_of(t * TILE, TILE), TILE)
@@ -176,23 +173,13 @@
             for n in range(negs):
                 ds = ds + jnp.where(hits[n], weights[n : n + 1, :], 0.0)
             ds = ((ds - jnp.where(first, total, 0.0)) * inv_root).astype(bf16)
-            dsc.append(ds)
+            dsc[lanes, :] = ds
             demb.append(dot(ds, cd, ((0,), (0,))))
         demb = jnp.concatenate(demb, axis=0)
         mean = jnp.mean(demb * embedding, axis=-1, keepdims=True)
         dhidden = scale * (demb - embedding * mean)
         dp = (dhidden * gate * (1.0 + preact * (1.0 - gate))).astype(bf16)
         dpre[at, :] = dp
-        own[pl.ds(c * (step // BLK), step // BLK)] = dot(dp, top, ((1,), (1,))).reshape(
-            step // BLK, BLK, width
-        )
-        dagg = (dot(dp, low, ((1,), (1,))) / degree).astype(bf16)
-        for tt in range(CHUNK):
-            t = c * CHUNK + tt
-            cd, ct = tiles[tt]
-            part = slice(tt * TILE, (tt + 1) * TILE)
-            got = dot(dsc[tt], half[part, :], ((1,), (0,))) + dot(ct, dagg[part, :], ((1,), (0,)))
-            dcand[pl.ds(t * NBT, NBT)] = got.reshape(NBT, BLK, width)
         return carry
 
     lax.fori_loop(0, rows // step, chunk, 0)
@@ -210,6 +197,35 @@
     keep[half_rows : half_rows + PAD, :] = spread
     send[half_rows : half_rows + PAD, :] = spread
 
+
+def tail_kernel(degree, where_own, where_slot, weight, counts, halves, dpre, dsc, own, *rest):
+    back, dcand = rest[:-1], rest[-1]
+    rows, width = dpre.shape
+    blocks = own.shape[0]
+    capacity = back[0].shape[0]
+    me = lax.axis_index("group")
+    top = weight[0:width, :]
+    low = weight[width : 2 * width, :]
+    step = CHUNK * TILE
+
+    def chunk(c, carry):
+        at = pl.ds(pl.multiple_of(c * step, step), step)
+        dp = dpre[at, :]
+        own[pl.ds(c * (step // BLK), step // BLK)] = dot(dp, top, ((1,), (1,))).reshape(
+            step // BLK, BLK, width
+        )
+        dagg = (dot(dp, low, ((1,), (1,))) / degree).astype(bf16)
+        for tt in range(CHUNK):
+            t = c * CHUNK + tt
+            lanes = pl.ds(pl.multiple_of(t * TILE, TILE), TILE)
+            part = slice(tt * TILE, (tt + 1) * TILE)
+            got = dot(dsc[lanes, :], halves[lanes, :], ((1,), (0,)))
+            got = got + dot(counts[lanes, :], dagg[part, :], ((1,), (0,)))
+            dcand[pl.ds(t * NBT, NBT)] = got.reshape(NBT, BLK, width)
+        return carry
+
+    lax.fori_loop(0, rows // step, chunk, 0)
+
     def scatter(i, carry):
         d = where_own[i]
         to = jnp.maximum(d, 0)
@@ -217,7 +233,7 @@
         return carry
 
     lax.fori_loop(0, blocks, scatter, 0, unroll=4)
-    for k in range(1, peers):
+    for k in range(1, len(back) + 1):
         base = (me ^ k) * capacity
 
         def outgo(c, carry, k=k, base=base):
@@ -288,6 +304,7 @@
         (boundary, request, blocks),
         [SMEM, SMEM, VMEM],
         VMEM,
+        limit=60,
     )
     pieces = {0: shared}
     bit = peers // 2
@@ -310,31 +327,34 @@
         (VMEM, VMEM, SMEM, SMEM),
         flops=2 * row_count * width * width * 8,
     )
-    outs = call(
+    wide = sds((row_count, width), bf16)
+    part = sds((width + PAD, width), f32)
+    keep, send, halves, dpre, dsc = call(
         functools.partial(main_kernel, peers),
-        (
-            sds((block_count, BLK, width), f32),
-            sds((width + PAD, width), f32),
-            sds((width + PAD, width), f32),
-        )
-        + (sds((capacity, BLK, width), f32),) * (peers - 1),
+        (part, part, wide, wide, sds((row_count, TILE), bf16)),
         (request, where_own, where_slot, blocks, layer_weight, nbr, neg, pre, counts)
         + tuple(pieces[k] for k in range(1, peers)),
         [SMEM] * 3 + [VMEM] * (5 + peers),
-        (VMEM,) * (peers + 2),
+        (VMEM,) * 5,
         scratch=(
             pltpu.VMEM((block_count, BLK, width), bf16),
             pltpu.VMEM((row_count, width), bf16),
-            pltpu.VMEM((row_count, width), bf16),
-            pltpu.VMEM((block_count, BLK, width), f32),
             pltpu.VMEM((2 * width, width), f32),
             pltpu.VMEM((8, TILE), f32),
         ),
-        flops=2 * row_count * width * width * 20,
-        limit=32,
-    )
-    own, keep, send = outs[:3]
-    back = outs[3:]
+        flops=2 * row_count * width * width * 16,
+        limit=24,
+    )
+    own, *back = call(
+        functools.partial(tail_kernel, nbr.shape[0]),
+        (sds((block_count, BLK, width), f32),) + (sds((capacity, BLK, width), f32),) * (peers - 1),
+        (where_own, where_slot, layer_weight, counts, halves, dpre, dsc),
+        [SMEM] * 2 + [VMEM] * 5,
+        (VMEM,) * peers,
+        scratch=(pltpu.VMEM((block_count, BLK, width), f32),),
+        flops=2 * row_count * width * width * 4,
+        limit=16,
+    )
 
     everyone = ("dom", "group")
 
@@ -346,7 +366,7 @@
         for k in range(1, peers)
     ]
     bits = [1 << b for b in range(1, devices.bit_length() - 1)]
-    masks = bits[-2:] + [bits[-3], bits[0]] + bits[1:-3]
+    masks = [bits[0], peers] + [b for b in bits[1:] if b != peers]
     stages = []
     for s in range(0, len(masks), 2):
         pair = (masks[s], masks[min(s + 1, len(masks) - 1)])

time: 86 us -> 90.4 us (1.051)
  Pallas kernels: 20.1 us -> 22.8 us
  local copies, waits for them, and re-layouts: 6.79 us -> 8.41 us
  other arithmetic: 0.1 us -> 1.72 us
  waiting for transfers between devices: 41.5 us -> 40.2 us
    ppermute x3, waiting for transfers between devices: 10.9 us -> 0.01 us  [per_device(): lax.ppermute(back[k - 1], 'group', [(i, i ^ k) for i in range(peers)])]
    ppermute x8, waiting for transfers between devices: 18.5 us -> 27.9 us  [swap(): lax.ppermute(x, everyone, [(i, i ^ masks[i & 1]) for i in range(devices)])]
    pallas_call x6 -> x7, Pallas kernels: 20.1 us -> 22.8 us  [call(): pl.pallas_call(kernel, out_shape=out_shape, in_specs=specs, out_specs=out...]
    unnamed x32, local copies, waits for them, and re-layouts: 6.04 us -> 8.36 us
    add x3, other arithmetic: 0.06 us -> 1.69 us  [per_device(): total = total + swap(total, pair)]
  transfers between devices with their start and end apart: 14 -> 14, of which waited for: 9 -> 6; matrix products, arithmetic and copies ran while one was open for 1% -> 1% of each run, Pallas kernels for 9% -> 13%
where the time goes in v3:
time: 90.4 us; the launch traced here: 89.9 us
  waiting for transfers between devices  40.2 us (44%)
  Pallas kernels  22.8 us (25%)
  starting transfers between devices  15.8 us (17%)
  local copies, waits for them, and re-layouts  8.41 us (9%)
  other arithmetic  1.72 us (2%)
    ppermute x8, waiting for transfers between devices, swap(): lax.ppermute(x, everyone, [(i, i ^ masks[i & 1]) for i in range(devices)])  27.9 us
    pallas_call x7, Pallas kernels, call(): pl.pallas_call(kernel, out_shape=out_shape, in_specs=specs, out_specs=out...  22.8 us
    ppermute x3, waiting for transfers between devices, per_device(): pieces[k | bit] = lax.ppermute(pieces[k], 'group', pairs)  12.3 us
    ppermute x8, starting transfers between devices, swap(): lax.ppermute(x, everyone, [(i, i ^ masks[i & 1]) for i in range(devices)])  10.9 us
    unnamed x32, local copies, waits for them, and re-layouts  8.36 us
    ppermute x3, starting transfers between devices, per_device(): pieces[k | bit] = lax.ppermute(pieces[k], 'group', pairs)  3 us
    ppermute x3, starting transfers between devices, per_device(): lax.ppermute(back[k - 1], 'group', [(i, i ^ k) for i in range(peers)])  1.92 us
  transfers between devices with their start and end apart: 14, of which 6 were waited for; matrix products, arithmetic and copies ran while one was open for 1% of the time, Pallas kernels for 13%

profile of v3, /device:TPU:0, one launch (start us, length us, event | category | flops | bytes accessed | tf_op | source)
XLA Modules:
  0.0 89.9 jit_solution(4161450305594656769)
XLA Ops:
  0.6 2.2 %shard_map.94 = bf16[65,16,256]{2,1,0:T(8,128)(2,1)} custom-call(s32[64]{0:T(128)} %boundary.5, s32[4,24]{1,0:T(4,128)} %request.5, bf16[128,16,256]{2,1,0:T(8,128)(2,1)} %bitcast.12), custom_call_target="tpu_custom_call" | custom-call | bytes 1049216 | tf_op jit(solution)/shard_map/pallas_call | solution.py:33
  2.9 3.0 %collective-permute-start.1 = (bf16[65,16,256]{2,1,0:T(8,128)(2,1)}, bf16[65,16,256]{2,1,0:T(8,128)(2,1)S(1)}, u32[]{:S(2)}, u32[]{:S(2)}) collective-permute-start(bf16[65,16,256]{2,1,0:T(8,128)(2,1)} %shard_map.94), channel_id=1, source_target_pairs={{0,2},{1,3},{2,0},{3,1},{4,6},{5,7},{6,4},{7,5},{8,10},{9,11},{10,... | collective-permute-start | bytes 1597448 | tf_op jit(solution)/shard_map/ppermute | solution.py:314
  5.9 12.3 %collective-permute-done.1.rest_1_ = bf16[65,16,256]{2,1,0:T(8,128)(2,1)S(1)} collective-permute-done((bf16[65,16,256]{2,1,0:T(8,128)(2,1)}, bf16[65,16,256]{2,1,0:T(8,128)(2,1)S(1)}, u32[]{:S(2)}, u32[]{:S(2)}) %collective-permute-start.1) | collective-permute-done | bytes 532512 | tf_op jit(solution)/shard_map/ppermute | solution.py:314
  18.2 1.2 %copy-done = bf16[2048,256]{1,0:T(8,128)(2,1)S(1)} copy-done((bf16[2048,256]{1,0:T(8,128)(2,1)S(1)}, bf16[2048,256]{1,0:T(8,128)(2,1)}, u32[]{:S(2)}) %copy-start) | copy-done | bytes 1048600
  19.4 0.7 copy-done.2
  20.1 0.7 copy-done.4
  20.7 0.9 %copy-done.6 = bf16[512,256]{1,0:T(8,128)(2,1)S(1)} copy-done((bf16[512,256]{1,0:T(8,128)(2,1)S(1)}, bf16[512,256]{1,0:T(8,128)(2,1)}, u32[]{:S(2)}) %copy-start.6) | copy-done | bytes 262168
  21.7 0.9 %copy-done.8 = s32[2048,10]{0,1:T(8,128)S(1)} copy-done((s32[2048,10]{0,1:T(8,128)S(1)}, s32[2048,10]{0,1:T(8,128)}, u32[]{:S(2)}) %copy-start.8) | copy-done | bytes 81944
  22.6 0.7 copy-done.11
  23.3 5.7 %shard_map.95 = (bf16[2048,128]{1,0:T(8,128)(2,1)S(1)}, f32[2048,256]{1,0:T(8,128)S(1)}, s32[128]{0:T(128)S(1)}, s32[97]{0:T(128)S(1)}) custom-call(s32[8,16]{1,0:T(8,128)S(1)} %bitcast.17, s32[4,24]{1,0:T(4,128)S(1)} %copy-done.2, s32[64]{0:T(128)S(1)} %copy-done.4, bf16[2048,256]{1,0:T(8,128)(2,1)S(1)} %copy-done, bf16[512,256]{1,0:T(8,128)(2,1)S(1)} %copy-done.6, ...), custom_call_target="tpu_custom_call" | custom-call | flops 2147483648 | bytes 1393792 | tf_op jit(solution)/shard_map/pallas_call | solution.py:33
  29.1 8.1 %shard_map.96 = (f32[264,256]{1,0:T(8,128)S(1)}, f32[264,256]{1,0:T(8,128)S(1)}, bf16[2048,256]{1,0:T(8,128)(2,1)S(1)}, bf16[2048,256]{1,0:T(8,128)(2,1)S(1)}, bf16[2048,128]{1,0:T(8,128)(2,1)S(1)}) custom-call(s32[4,24]{1,0:T(4,128)S(1)} %copy-done.3, s32[128]{0:T(128)S(1)} %get-tuple-element.20.where_own, s32[97]{0:T(128)S(1)} %get-tuple-element.21.where_slot, ...), custom_call_target="tpu_custom_call" | custom-call | flops 4294967296 | bytes 5645572 | tf_op jit(solution)/shard_map/pallas_call | solution.py:33
  37.2 1.0 %copy-done.12 = bf16[2048,256]{1,0:T(8,128)(2,1)} copy-done((bf16[2048,256]{1,0:T(8,128)(2,1)}, bf16[2048,256]{1,0:T(8,128)(2,1)S(1)}, u32[]{:S(2)}) %copy-start.12) | copy-done | bytes 1048600
  38.1 0.5 collective-permute-start.6
  38.6 1.2 %collective-permute-done.6.other = f32[264,256]{1,0:T(8,128)S(1)} collective-permute-done((f32[264,256]{1,0:T(8,128)S(1)}, f32[264,256]{1,0:T(8,128)S(1)}, u32[]{:S(2)}, u32[]{:S(2)}) %collective-permute-start.6) | collective-permute-done | bytes 270368 | tf_op jit(solution)/shard_map/ppermute | solution.py:362
  39.8 1.8 %collective-permute-start.7 = (f32[136,256]{1,0:T(8,128)S(1)}, f32[136,256]{1,0:T(8,128)S(1)}, u32[]{:S(2)}, u32[]{:S(2)}) collective-permute-start(f32[136,256]{1,0:T(8,128)S(1)} %get-tuple-element.34), channel_id=1, source_target_pairs={{0,2},{1,5},{2,0},{3,7},{4,6},{5,1},{6,4},{7,3},{8,10},{9,13},{10,... | collective-permute-start | bytes 417800 | tf_op jit(solution)/shard_map/ppermute | solution.py:362
  41.6 3.3 %collective-permute-done.7 = f32[136,256]{1,0:T(8,128)S(1)} collective-permute-done((f32[136,256]{1,0:T(8,128)S(1)}, f32[136,256]{1,0:T(8,128)S(1)}, u32[]{:S(2)}, u32[]{:S(2)}) %collective-permute-start.7) | collective-permute-done | bytes 139296 | tf_op jit(solution)/shard_map/ppermute | solution.py:362
  45.0 1.8 %collective-permute-start.8 = (f32[136,256]{1,0:T(8,128)S(1)}, f32[136,256]{1,0:T(8,128)S(1)}, u32[]{:S(2)}, u32[]{:S(2)}) collective-permute-start(f32[136,256]{1,0:T(8,128)S(1)} %add.18), channel_id=1, source_target_pairs={{0,4},{1,3},{2,6},{3,1},{4,0},{5,7},{6,2},{7,5},{8,12},{9,11},{10,... | collective-permute-start | bytes 417800 | tf_op jit(solution)/shard_map/ppermute | solution.py:362
  46.8 3.3 %collective-permute-done.8 = f32[136,256]{1,0:T(8,128)S(1)} collective-permute-done((f32[136,256]{1,0:T(8,128)S(1)}, f32[136,256]{1,0:T(8,128)S(1)}, u32[]{:S(2)}, u32[]{:S(2)}) %collective-permute-start.8) | collective-permute-done | bytes 139296 | tf_op jit(solution)/shard_map/ppermute | solution.py:362
  50.1 1.9 %collective-permute-start.9 = (f32[136,256]{1,0:T(8,128)S(1)}, f32[136,256]{1,0:T(8,128)S(1)}, u32[]{:S(2)}, u32[]{:S(2)}) collective-permute-start(f32[136,256]{1,0:T(8,128)S(1)} %add.19), channel_id=1, source_target_pairs={{0,8},{1,17},{2,10},{3,19},{4,12},{5,21},{6,14},{7,23},{8,0},{9,25... | collective-permute-start | bytes 417800 | tf_op jit(solution)/shard_map/ppermute | solution.py:362
  52.0 3.3 %collective-permute-done.9 = f32[136,256]{1,0:T(8,128)S(1)} collective-permute-done((f32[136,256]{1,0:T(8,128)S(1)}, f32[136,256]{1,0:T(8,128)S(1)}, u32[]{:S(2)}, u32[]{:S(2)}) %collective-permute-start.9) | collective-permute-done | bytes 139296 | tf_op jit(solution)/shard_map/ppermute | solution.py:362
  55.3 0.7 add.20
  55.9 3.3 %collective-permute-start.10 = (f32[136,256]{1,0:T(8,128)}, f32[136,256]{1,0:T(8,128)}, u32[]{:S(2)}, u32[]{:S(2)}) collective-permute-start(f32[136,256]{1,0:T(8,128)} %add.20), channel_id=1, source_target_pairs={{0,16},{1,9},{2,18},{3,11},{4,20},{5,13},{6,22},{7,15},{8,24},{9,1... | collective-permute-start | bytes 417800 | tf_op jit(solution)/shard_map/ppermute | solution.py:362
  59.2 1.2 %copy-done.13 = bf16[2048,256]{1,0:T(8,128)(2,1)S(1)} copy-done((bf16[2048,256]{1,0:T(8,128)(2,1)S(1)}, bf16[2048,256]{1,0:T(8,128)(2,1)}, u32[]{:S(2)}) %copy-start.13) | copy-done | bytes 1048600
  60.4 1.0 %copy-done.15 = bf16[2048,128]{1,0:T(8,128)(2,1)S(1)} copy-done((bf16[2048,128]{1,0:T(8,128)(2,1)S(1)}, bf16[2048,128]{1,0:T(8,128)(2,1)}, u32[]{:S(2)}) %copy-start.15) | copy-done | bytes 524312
  61.5 3.5 %shard_map.97 = (f32[128,16,256]{2,1,0:T(8,128)S(1)}, f32[24,16,256]{2,1,0:T(8,128)S(1)}, f32[24,16,256]{2,1,0:T(8,128)S(1)}, f32[24,16,256]{2,1,0:T(8,128)S(1)}) custom-call(s32[128]{0:T(128)S(1)} %get-tuple-element.20.where_own, s32[97]{0:T(128)S(1)} %get-tuple-element.21.where_slot, bf16[512,256]{1,0:T(8,128)(2,1)S(1)} %copy-done.7, ...), custom_call_target="tpu_custom_call" | custom-call | flops 1073741824 | bytes 3408772 | tf_op jit(solution)/shard_map/pallas_call | solution.py:33
  65.1 1.6 %collective-permute-start.4 = (f32[24,16,256]{2,1,0:T(8,128)S(1)}, f32[24,16,256]{2,1,0:T(8,128)S(1)}, u32[]{:S(2)}, u32[]{:S(2)}) collective-permute-start(f32[24,16,256]{2,1,0:T(8,128)S(1)} %get-tuple-element.29), channel_id=1, source_target_pairs={{0,2},{1,3},{2,0},{3,1},{4,6},{5,7},{6,4},{7,5},{8,10},{9,11},{10,... | collective-permute-start | bytes 1179656 | tf_op jit(solution)/shard_map/ppermute | solution.py:365
  66.7 0.2 collective-permute-start.5
  66.9 1.0 %add.21.mine = f32[136,256]{1,0:T(8,128)S(1)} add(f32[136,256]{1,0:T(8,128)} %add.20, f32[136,256]{1,0:T(8,128)} %collective-permute-done.10) | non-fusion elementwise | flops 34816 | bytes 417792 | tf_op jit(solution)/shard_map/add | solution.py:385
  67.9 1.6 %collective-permute-start.11 = (f32[136,256]{1,0:T(8,128)S(1)}, f32[136,256]{1,0:T(8,128)S(1)}, u32[]{:S(2)}, u32[]{:S(2)}) collective-permute-start(f32[136,256]{1,0:T(8,128)S(1)} %add.21.mine), channel_id=1, source_target_pairs={{0,2},{1,5},{2,0},{3,7},{4,6},{5,1},{6,4},{7,3},{8,10},{9,13},{10,... | collective-permute-start | bytes 417800 | tf_op jit(solution)/shard_map/ppermute | solution.py:362
  69.7 16.8 %collective-permute-done.11.far = f32[136,256]{1,0:T(8,128)S(1)} collective-permute-done((f32[136,256]{1,0:T(8,128)S(1)}, f32[136,256]{1,0:T(8,128)S(1)}, u32[]{:S(2)}, u32[]{:S(2)}) %collective-permute-start.11) | collective-permute-done | bytes 139296 | tf_op jit(solution)/shard_map/ppermute | solution.py:362
  86.6 2.4 %shard_map.98 = f32[128,16,256]{2,1,0:T(8,128)} custom-call(s32[64]{0:T(128)S(1)} %copy-done.5, s32[3,24]{1,0:T(4,128)S(1)} %maximum_convert_fusion.asked, f32[128,16,256]{2,1,0:T(8,128)S(1)} %get-tuple-element.27.own_in, f32[24,16,256]{2,1,0:T(8,128)S(1)} %collective-permute-done.3.rest_0_, f32[24,16,256]{2,1,0:T(8,128)S(1)} %collective-permute-done.4.rest_1_, ...), custom_call_target="tpu_custom_call" | custom-call | bytes 3277344 | tf_op jit(solution)/shard_map/pallas_call | solution.py:33
  89.0 0.9 shard_map.100
  (49 shorter events, 0.4 us)
Async XLA Ops:
  2.9 15.3 %collective-permute-start.1 = (bf16[65,16,256]{2,1,0:T(8,128)(2,1)}, bf16[65,16,256]{2,1,0:T(8,128)(2,1)S(1)}, u32[]{:S(2)}, u32[]{:S(2)}) collective-permute-start(bf16[65,16,256]{2,1,0:T(8,128)(2,1)} %shard_map.94), channel_id=1, source_target_pairs={{0,2},{1,3},{2,0},{3,1},{4,6},{5,7},{6,4},{7,5},{8,10},{9,11},{10,... | collective-permute-start | bytes 1597448 | tf_op jit(solution)/shard_map/ppermute | solution.py:314
  5.9 23.1 %collective-permute-start = (bf16[65,16,256]{2,1,0:T(8,128)(2,1)}, bf16[65,16,256]{2,1,0:T(8,128)(2,1)S(1)}, u32[]{:S(2)}, u32[]{:S(2)}) collective-permute-start(bf16[65,16,256]{2,1,0:T(8,128)(2,1)} %shard_map.94), channel_id=1, source_target_pairs={{0,1},{1,0},{2,3},{3,2},{4,5},{5,4},{6,7},{7,6},{8,9},{9,8},{10,11... | collective-permute-start | bytes 1597448 | tf_op jit(solution)/shard_map/ppermute | solution.py:314
  18.2 10.8 %collective-permute-start.2 = (bf16[65,16,256]{2,1,0:T(8,128)(2,1)S(1)}, bf16[65,16,256]{2,1,0:T(8,128)(2,1)S(1)}, u32[]{:S(2)}, u32[]{:S(2)}) collective-permute-start(bf16[65,16,256]{2,1,0:T(8,128)(2,1)S(1)} %collective-permute-done.1.rest_1_), channel_id=1, source_target_pairs={{0,1},{1,0},{2,3},{3,2},{4,5},{5,4},{6,7},{7,6},{8,9},{9,8},{10,11... | collective-permute-start | bytes 1597448 | tf_op jit(solution)/shard_map/ppermute | solution.py:314
  18.2 1.2 %copy-start = (bf16[2048,256]{1,0:T(8,128)(2,1)S(1)}, bf16[2048,256]{1,0:T(8,128)(2,1)}, u32[]{:S(2)}) copy-start(bf16[2048,256]{1,0:T(8,128)(2,1)} %feat.1) | copy-start | bytes 3145732
  19.4 0.7 copy-start.2
  20.1 0.7 copy-start.4
  20.7 0.9 %copy-start.6 = (bf16[512,256]{1,0:T(8,128)(2,1)S(1)}, bf16[512,256]{1,0:T(8,128)(2,1)}, u32[]{:S(2)}) copy-start(bf16[512,256]{1,0:T(8,128)(2,1)} %weight.5) | copy-start | bytes 786436
  21.7 0.9 %copy-start.8 = (s32[2048,10]{0,1:T(8,128)S(1)}, s32[2048,10]{0,1:T(8,128)}, u32[]{:S(2)}) copy-start(s32[2048,10]{0,1:T(8,128)} %param.11) | copy-start | bytes 245764
  22.6 0.7 copy-start.11
  23.3 5.7 %copy-start.1 = (bf16[2048,256]{1,0:T(8,128)(2,1)S(1)}, bf16[2048,256]{1,0:T(8,128)(2,1)}, u32[]{:S(2)}) copy-start(bf16[2048,256]{1,0:T(8,128)(2,1)} %feat.1) | copy-start | bytes 3145732
  23.3 5.7 %copy-start.3 = (s32[4,24]{1,0:T(4,128)S(1)}, s32[4,24]{1,0:T(4,128)}, u32[]{:S(2)}) copy-start(s32[4,24]{1,0:T(4,128)} %request.5) | copy-start | bytes 1156
  23.3 5.8 %copy-start.7 = (bf16[512,256]{1,0:T(8,128)(2,1)S(1)}, bf16[512,256]{1,0:T(8,128)(2,1)}, u32[]{:S(2)}) copy-start(bf16[512,256]{1,0:T(8,128)(2,1)} %weight.5) | copy-start | bytes 786436
  23.3 5.8 %copy-start.9 = (s32[2048,10]{0,1:T(8,128)S(1)}, s32[2048,10]{0,1:T(8,128)}, u32[]{:S(2)}) copy-start(s32[2048,10]{0,1:T(8,128)} %param.11) | copy-start | bytes 245764
  23.3 5.8 %copy-start.10 = (s32[2048,4]{0,1:T(4,128)S(1)}, s32[2048,4]{0,1:T(4,128)}, u32[]{:S(2)}) copy-start(s32[2048,4]{0,1:T(4,128)} %param.12) | copy-start | bytes 98308
  37.2 1.0 %copy-start.12 = (bf16[2048,256]{1,0:T(8,128)(2,1)}, bf16[2048,256]{1,0:T(8,128)(2,1)S(1)}, u32[]{:S(2)}) copy-start(bf16[2048,256]{1,0:T(8,128)(2,1)S(1)} %get-tuple-element.25.dpre) | copy-start | bytes 3145732
  38.1 6.9 %copy-start.14 = (bf16[2048,128]{1,0:T(8,128)(2,1)}, bf16[2048,128]{1,0:T(8,128)(2,1)S(1)}, u32[]{:S(2)}) copy-start(bf16[2048,128]{1,0:T(8,128)(2,1)S(1)} %get-tuple-element.26.dsc) | copy-start | bytes 1572868
  38.1 1.7 %collective-permute-start.6 = (f32[264,256]{1,0:T(8,128)S(1)}, f32[264,256]{1,0:T(8,128)S(1)}, u32[]{:S(2)}, u32[]{:S(2)}) collective-permute-start(f32[264,256]{1,0:T(8,128)S(1)} %get-tuple-element.32), channel_id=1, source_target_pairs={{0,1},{1,0},{2,3},{3,2},{4,5},{5,4},{6,7},{7,6},{8,9},{9,8},{10,11... | collective-permute-start | bytes 811016 | tf_op jit(solution)/shard_map/ppermute | solution.py:362
  39.8 5.1 %collective-permute-start.7 = (f32[136,256]{1,0:T(8,128)S(1)}, f32[136,256]{1,0:T(8,128)S(1)}, u32[]{:S(2)}, u32[]{:S(2)}) collective-permute-start(f32[136,256]{1,0:T(8,128)S(1)} %get-tuple-element.34), channel_id=1, source_target_pairs={{0,2},{1,5},{2,0},{3,7},{4,6},{5,1},{6,4},{7,3},{8,10},{9,13},{10,... | collective-permute-start | bytes 417800 | tf_op jit(solution)/shard_map/ppermute | solution.py:362
  45.0 5.1 %collective-permute-start.8 = (f32[136,256]{1,0:T(8,128)S(1)}, f32[136,256]{1,0:T(8,128)S(1)}, u32[]{:S(2)}, u32[]{:S(2)}) collective-permute-start(f32[136,256]{1,0:T(8,128)S(1)} %add.18), channel_id=1, source_target_pairs={{0,4},{1,3},{2,6},{3,1},{4,0},{5,7},{6,2},{7,5},{8,12},{9,11},{10,... | collective-permute-start | bytes 417800 | tf_op jit(solution)/shard_map/ppermute | solution.py:362
  50.1 5.1 %collective-permute-start.9 = (f32[136,256]{1,0:T(8,128)S(1)}, f32[136,256]{1,0:T(8,128)S(1)}, u32[]{:S(2)}, u32[]{:S(2)}) collective-permute-start(f32[136,256]{1,0:T(8,128)S(1)} %add.19), channel_id=1, source_target_pairs={{0,8},{1,17},{2,10},{3,19},{4,12},{5,21},{6,14},{7,23},{8,0},{9,25... | collective-permute-start | bytes 417800 | tf_op jit(solution)/shard_map/ppermute | solution.py:362
  55.9 11.0 %collective-permute-start.10 = (f32[136,256]{1,0:T(8,128)}, f32[136,256]{1,0:T(8,128)}, u32[]{:S(2)}, u32[]{:S(2)}) collective-permute-start(f32[136,256]{1,0:T(8,128)} %add.20), channel_id=1, source_target_pairs={{0,16},{1,9},{2,18},{3,11},{4,20},{5,13},{6,22},{7,15},{8,24},{9,1... | collective-permute-start | bytes 417800 | tf_op jit(solution)/shard_map/ppermute | solution.py:362
  59.2 1.2 %copy-start.13 = (bf16[2048,256]{1,0:T(8,128)(2,1)S(1)}, bf16[2048,256]{1,0:T(8,128)(2,1)}, u32[]{:S(2)}) copy-start(bf16[2048,256]{1,0:T(8,128)(2,1)} %copy-done.12) | copy-start | bytes 3145732
  60.4 1.0 %copy-start.15 = (bf16[2048,128]{1,0:T(8,128)(2,1)S(1)}, bf16[2048,128]{1,0:T(8,128)(2,1)}, u32[]{:S(2)}) copy-start(bf16[2048,128]{1,0:T(8,128)(2,1)} %copy-done.14) | copy-start | bytes 1572868
  61.5 25.1 %copy-start.5 = (s32[64]{0:T(128)S(1)}, s32[64]{0:T(128)}, u32[]{:S(2)}) copy-start(s32[64]{0:T(128)} %boundary.5) | copy-start | bytes 772
  65.0 21.6 %collective-permute-start.3 = (f32[24,16,256]{2,1,0:T(8,128)S(1)}, f32[24,16,256]{2,1,0:T(8,128)S(1)}, u32[]{:S(2)}, u32[]{:S(2)}) collective-permute-start(f32[24,16,256]{2,1,0:T(8,128)S(1)} %get-tuple-element.28), channel_id=1, source_target_pairs={{0,1},{1,0},{2,3},{3,2},{4,5},{5,4},{6,7},{7,6},{8,9},{9,8},{10,11... | collective-permute-start | bytes 1179656 | tf_op jit(solution)/shard_map/ppermute | solution.py:365
  65.1 21.5 %collective-permute-start.4 = (f32[24,16,256]{2,1,0:T(8,128)S(1)}, f32[24,16,256]{2,1,0:T(8,128)S(1)}, u32[]{:S(2)}, u32[]{:S(2)}) collective-permute-start(f32[24,16,256]{2,1,0:T(8,128)S(1)} %get-tuple-element.29), channel_id=1, source_target_pairs={{0,2},{1,3},{2,0},{3,1},{4,6},{5,7},{6,4},{7,5},{8,10},{9,11},{10,... | collective-permute-start | bytes 1179656 | tf_op jit(solution)/shard_map/ppermute | solution.py:365
  66.7 19.9 %collective-permute-start.5 = (f32[24,16,256]{2,1,0:T(8,128)S(1)}, f32[24,16,256]{2,1,0:T(8,128)S(1)}, u32[]{:S(2)}, u32[]{:S(2)}) collective-permute-start(f32[24,16,256]{2,1,0:T(8,128)S(1)} %get-tuple-element.30), channel_id=1, source_target_pairs={{0,3},{1,2},{2,1},{3,0},{4,7},{5,6},{6,5},{7,4},{8,11},{9,10},{10,... | collective-permute-start | bytes 1179656 | tf_op jit(solution)/shard_map/ppermute | solution.py:365
  67.9 18.6 %collective-permute-start.11 = (f32[136,256]{1,0:T(8,128)S(1)}, f32[136,256]{1,0:T(8,128)S(1)}, u32[]{:S(2)}, u32[]{:S(2)}) collective-permute-start(f32[136,256]{1,0:T(8,128)S(1)} %add.21.mine), channel_id=1, source_target_pairs={{0,2},{1,5},{2,0},{3,7},{4,6},{5,1},{6,4},{7,3},{8,10},{9,13},{10,... | collective-permute-start | bytes 417800 | tf_op jit(solution)/shard_map/ppermute | solution.py:362
  69.6 19.4 %collective-permute-start.12 = (f32[136,256]{1,0:T(8,128)S(1)}, f32[136,256]{1,0:T(8,128)S(1)}, u32[]{:S(2)}, u32[]{:S(2)}) collective-permute-start(f32[136,256]{1,0:T(8,128)S(1)} %add.21.mine), channel_id=1, source_target_pairs={{0,1},{1,0},{2,3},{3,2},{4,5},{5,4},{6,7},{7,6},{8,9},{9,8},{10,11... | collective-permute-start | bytes 417800 | tf_op jit(solution)/shard_map/ppermute | solution.py:362
  86.5 2.5 %collective-permute-start.13 = (f32[136,256]{1,0:T(8,128)S(1)}, f32[136,256]{1,0:T(8,128)S(1)}, u32[]{:S(2)}, u32[]{:S(2)}) collective-permute-start(f32[136,256]{1,0:T(8,128)S(1)} %collective-permute-done.11.far), channel_id=1, source_target_pairs={{0,1},{1,0},{2,3},{3,2},{4,5},{5,4},{6,7},{7,6},{8,9},{9,8},{10,11... | collective-permute-start | bytes 417800 | tf_op jit(solution)/shard_map/ppermute | solution.py:362

commit v4 on v3

--- a/solution.py
+++ b/solution.py
@@ -198,14 +198,26 @@
     send[half_rows : half_rows + PAD, :] = spread
 
 
-def tail_kernel(degree, where_own, where_slot, weight, counts, halves, dpre, dsc, own, *rest):
+def agg_kernel(degree, weight, dpre, dagg):
+    rows, width = dpre.shape
+    low = weight[width : 2 * width, :]
+    step = CHUNK * TILE
+
+    def chunk(c, carry):
+        at = pl.ds(pl.multiple_of(c * step, step), step)
+        dagg[at, :] = (dot(dpre[at, :], low, ((1,), (1,))) / degree).astype(bf16)
+        return carry
+
+    lax.fori_loop(0, rows // step, chunk, 0)
+
+
+def tail_kernel(where_own, where_slot, weight, counts, halves, dpre, dsc, dagg, own, *rest):
     back, dcand = rest[:-1], rest[-1]
     rows, width = dpre.shape
     blocks = own.shape[0]
     capacity = back[0].shape[0]
     me = lax.axis_index("group")
     top = weight[0:width, :]
-    low = weight[width : 2 * width, :]
     step = CHUNK * TILE
 
     def chunk(c, carry):
@@ -214,13 +226,11 @@
         own[pl.ds(c * (step // BLK), step // BLK)] = dot(dp, top, ((1,), (1,))).reshape(
             step // BLK, BLK, width
         )
-        dagg = (dot(dp, low, ((1,), (1,))) / degree).astype(bf16)
         for tt in range(CHUNK):
             t = c * CHUNK + tt
             lanes = pl.ds(pl.multiple_of(t * TILE, TILE), TILE)
-            part = slice(tt * TILE, (tt + 1) * TILE)
             got = dot(dsc[lanes, :], halves[lanes, :], ((1,), (0,)))
-            got = got + dot(counts[lanes, :], dagg[part, :], ((1,), (0,)))
+            got = got + dot(counts[lanes, :], dagg[lanes, :], ((1,), (0,)))
             dcand[pl.ds(t * NBT, NBT)] = got.reshape(NBT, BLK, width)
         return carry
 
@@ -345,11 +355,19 @@
         flops=2 * row_count * width * width * 16,
         limit=24,
     )
+    dagg = call(
+        functools.partial(agg_kernel, nbr.shape[0]),
+        wide,
+        (layer_weight, dpre),
+        [VMEM] * 2,
+        VMEM,
+        flops=2 * row_count * width * width,
+    )
     own, *back = call(
-        functools.partial(tail_kernel, nbr.shape[0]),
+        tail_kernel,
         (sds((block_count, BLK, width), f32),) + (sds((capacity, BLK, width), f32),) * (peers - 1),
-        (where_own, where_slot, layer_weight, counts, halves, dpre, dsc),
-        [SMEM] * 2 + [VMEM] * 5,
+        (where_own, where_slot, layer_weight, counts, halves, dpre, dsc, dagg),
+        [SMEM] * 2 + [VMEM] * 6,
         (VMEM,) * peers,
         scratch=(pltpu.VMEM((block_count, BLK, width), f32),),
         flops=2 * row_count * width * width * 4,
@@ -385,7 +403,7 @@
         total = total + swap(total, pair)
     far = swap(total, split)
     theirs = swap(total, (1, 1))
-    theirs_far = swap(far, (1, 1))
+    theirs_far = swap(total, (split[0] ^ 1, split[1] ^ 1))
     weight_grad, loss = call(
         functools.partial(finish_kernel, split, row_count, row_count * devices),
         (sds((2 * width, width), f32), sds((1, 1), f32)),

time: 90.4 us -> 79.2 us (0.88)
  waiting for transfers between devices: 40.2 us -> 29.9 us
  local copies, waits for them, and re-layouts: 8.41 us -> 6.82 us
  Pallas kernels: 22.8 us -> 24 us
    ppermute x8, waiting for transfers between devices: 27.9 us -> 11.4 us  [swap(): lax.ppermute(x, everyone, [(i, i ^ masks[i & 1]) for i in range(devices)])]
    ppermute x3, waiting for transfers between devices: 0.01 us -> 6.17 us  [per_device(): lax.ppermute(back[k - 1], 'group', [(i, i ^ k) for i in range(peers)])]
    unnamed x32 -> x30, local copies, waits for them, and re-layouts: 8.36 us -> 6.07 us
    pallas_call x7 -> x8, Pallas kernels: 22.8 us -> 24 us  [call(): pl.pallas_call(kernel, out_shape=out_shape, in_specs=specs, out_specs=out...]
    ppermute x8, starting transfers between devices: 10.9 us -> 9.97 us  [swap(): lax.ppermute(x, everyone, [(i, i ^ masks[i & 1]) for i in range(devices)])]
  transfers between devices with their start and end apart: 14 -> 14, of which waited for: 6 -> 7; matrix products, arithmetic and copies ran while one was open for 1% -> 3% of each run, Pallas kernels for 13% -> 16%
where the time goes in v4:
time: 79.2 us; the launch traced here: 78.9 us
  waiting for transfers between devices  29.9 us (38%)
  Pallas kernels  24 us (30%)
  starting transfers between devices  15.6 us (20%)
  local copies, waits for them, and re-layouts  6.82 us (9%)
  other arithmetic  1.72 us (2%)
  between operations  0.83 us (1%)
    pallas_call x8, Pallas kernels, call(): pl.pallas_call(kernel, out_shape=out_shape, in_specs=specs, out_specs=out...  24 us
    ppermute x3, waiting for transfers between devices, per_device(): pieces[k | bit] = lax.ppermute(pieces[k], 'group', pairs)  12.3 us
    ppermute x8, waiting for transfers between devices, swap(): lax.ppermute(x, everyone, [(i, i ^ masks[i & 1]) for i in range(devices)])  11.4 us
    ppermute x8, starting transfers between devices, swap(): lax.ppermute(x, everyone, [(i, i ^ masks[i & 1]) for i in range(devices)])  9.97 us
    ppermute x3, waiting for transfers between devices, per_device(): lax.ppermute(back[k - 1], 'group', [(i, i ^ k) for i in range(peers)])  6.17 us
    unnamed x30, local copies, waits for them, and re-layouts  6.07 us
    ppermute x3, starting transfers between devices, per_device(): pieces[k | bit] = lax.ppermute(pieces[k], 'group', pairs)  3 us
    ppermute x3, starting transfers between devices, per_device(): lax.ppermute(back[k - 1], 'group', [(i, i ^ k) for i in range(peers)])  2.61 us
  transfers between devices with their start and end apart: 14, of which 7 were waited for; matrix products, arithmetic and copies ran while one was open for 3% of the time, Pallas kernels for 16%

profile of v4, /device:TPU:0, one launch (start us, length us, event | category | flops | bytes accessed | tf_op | source)
XLA Modules:
  0.0 78.9 jit_solution(17340310905838283664)
XLA Ops:
  0.6 2.2 %shard_map.94 = bf16[65,16,256]{2,1,0:T(8,128)(2,1)} custom-call(s32[64]{0:T(128)} %boundary.5, s32[4,24]{1,0:T(4,128)} %request.5, bf16[128,16,256]{2,1,0:T(8,128)(2,1)} %bitcast.12), custom_call_target="tpu_custom_call" | custom-call | bytes 1049216 | tf_op jit(solution)/shard_map/pallas_call | solution.py:33
  2.9 3.0 %collective-permute-start.1 = (bf16[65,16,256]{2,1,0:T(8,128)(2,1)}, bf16[65,16,256]{2,1,0:T(8,128)(2,1)S(1)}, u32[]{:S(2)}, u32[]{:S(2)}) collective-permute-start(bf16[65,16,256]{2,1,0:T(8,128)(2,1)} %shard_map.94), channel_id=1, source_target_pairs={{0,2},{1,3},{2,0},{3,1},{4,6},{5,7},{6,4},{7,5},{8,10},{9,11},{10,... | collective-permute-start | bytes 1597448 | tf_op jit(solution)/shard_map/ppermute | solution.py:324
  5.9 12.3 %collective-permute-done.1.rest_1_ = bf16[65,16,256]{2,1,0:T(8,128)(2,1)S(1)} collective-permute-done((bf16[65,16,256]{2,1,0:T(8,128)(2,1)}, bf16[65,16,256]{2,1,0:T(8,128)(2,1)S(1)}, u32[]{:S(2)}, u32[]{:S(2)}) %collective-permute-start.1) | collective-permute-done | bytes 532512 | tf_op jit(solution)/shard_map/ppermute | solution.py:324
  18.2 1.1 %copy-done = bf16[512,256]{1,0:T(8,128)(2,1)S(1)} copy-done((bf16[512,256]{1,0:T(8,128)(2,1)S(1)}, bf16[512,256]{1,0:T(8,128)(2,1)}, u32[]{:S(2)}) %copy-start) | copy-done | bytes 262168
  19.3 1.2 %copy-done.2 = bf16[2048,256]{1,0:T(8,128)(2,1)S(1)} copy-done((bf16[2048,256]{1,0:T(8,128)(2,1)S(1)}, bf16[2048,256]{1,0:T(8,128)(2,1)}, u32[]{:S(2)}) %copy-start.2) | copy-done | bytes 1048600
  20.5 0.7 copy-done.4
  21.2 0.7 copy-done.6
  21.9 0.9 %copy-done.11 = s32[2048,10]{0,1:T(8,128)S(1)} copy-done((s32[2048,10]{0,1:T(8,128)S(1)}, s32[2048,10]{0,1:T(8,128)}, u32[]{:S(2)}) %copy-start.11) | copy-done | bytes 81944
  22.8 0.7 copy-done.14
  23.5 5.7 %shard_map.95 = (bf16[2048,128]{1,0:T(8,128)(2,1)S(1)}, f32[2048,256]{1,0:T(8,128)S(1)}, s32[128]{0:T(128)S(1)}, s32[97]{0:T(128)S(1)}) custom-call(s32[8,16]{1,0:T(8,128)S(1)} %bitcast.17, s32[4,24]{1,0:T(4,128)S(1)} %copy-done.4, s32[64]{0:T(128)S(1)} %copy-done.6, bf16[2048,256]{1,0:T(8,128)(2,1)S(1)} %copy-done.2, bf16[512,256]{1,0:T(8,128)(2,1)S(1)} %copy-done, ...), custom_call_target="tpu_custom_call" | custom-call | flops 2147483648 | bytes 1393792 | tf_op jit(solution)/shard_map/pallas_call | solution.py:33
  29.3 8.1 %shard_map.96 = (f32[264,256]{1,0:T(8,128)S(1)}, f32[264,256]{1,0:T(8,128)S(1)}, bf16[2048,256]{1,0:T(8,128)(2,1)S(1)}, bf16[2048,256]{1,0:T(8,128)(2,1)S(1)}, bf16[2048,128]{1,0:T(8,128)(2,1)S(1)}) custom-call(s32[4,24]{1,0:T(4,128)S(1)} %copy-done.5, s32[128]{0:T(128)S(1)} %get-tuple-element.20.where_own, s32[97]{0:T(128)S(1)} %get-tuple-element.21.where_slot, ...), custom_call_target="tpu_custom_call" | custom-call | flops 4294967296 | bytes 5645572 | tf_op jit(solution)/shard_map/pallas_call | solution.py:33
  37.8 1.2 %collective-permute-done.6.other = f32[264,256]{1,0:T(8,128)S(1)} collective-permute-done((f32[264,256]{1,0:T(8,128)S(1)}, f32[264,256]{1,0:T(8,128)S(1)}, u32[]{:S(2)}, u32[]{:S(2)}) %collective-permute-start.6) | collective-permute-done | bytes 270368 | tf_op jit(solution)/shard_map/ppermute | solution.py:380
  39.0 1.8 %collective-permute-start.7 = (f32[136,256]{1,0:T(8,128)S(1)}, f32[136,256]{1,0:T(8,128)S(1)}, u32[]{:S(2)}, u32[]{:S(2)}) collective-permute-start(f32[136,256]{1,0:T(8,128)S(1)} %get-tuple-element.34), channel_id=1, source_target_pairs={{0,2},{1,5},{2,0},{3,7},{4,6},{5,1},{6,4},{7,3},{8,10},{9,13},{10,... | collective-permute-start | bytes 417800 | tf_op jit(solution)/shard_map/ppermute | solution.py:380
  40.8 3.3 %collective-permute-done.7 = f32[136,256]{1,0:T(8,128)S(1)} collective-permute-done((f32[136,256]{1,0:T(8,128)S(1)}, f32[136,256]{1,0:T(8,128)S(1)}, u32[]{:S(2)}, u32[]{:S(2)}) %collective-permute-start.7) | collective-permute-done | bytes 139296 | tf_op jit(solution)/shard_map/ppermute | solution.py:380
  44.2 1.8 %collective-permute-start.8 = (f32[136,256]{1,0:T(8,128)S(1)}, f32[136,256]{1,0:T(8,128)S(1)}, u32[]{:S(2)}, u32[]{:S(2)}) collective-permute-start(f32[136,256]{1,0:T(8,128)S(1)} %add.18), channel_id=1, source_target_pairs={{0,4},{1,3},{2,6},{3,1},{4,0},{5,7},{6,2},{7,5},{8,12},{9,11},{10,... | collective-permute-start | bytes 417800 | tf_op jit(solution)/shard_map/ppermute | solution.py:380
  45.9 1.1 %shard_map.97.dagg = bf16[2048,256]{1,0:T(8,128)(2,1)S(1)} custom-call(bf16[512,256]{1,0:T(8,128)(2,1)S(1)} %copy-done.1, bf16[2048,256]{1,0:T(8,128)(2,1)S(1)} %get-tuple-element.25.dpre), custom_call_target="tpu_custom_call" | custom-call | flops 268435456 | bytes 1310720 | tf_op jit(solution)/shard_map/pallas_call | solution.py:33
  47.0 3.6 %shard_map.98 = (f32[128,16,256]{2,1,0:T(8,128)S(1)}, f32[24,16,256]{2,1,0:T(8,128)}, f32[24,16,256]{2,1,0:T(8,128)S(1)}, f32[24,16,256]{2,1,0:T(8,128)S(1)}) custom-call(s32[128]{0:T(128)S(1)} %get-tuple-element.20.where_own, s32[97]{0:T(128)S(1)} %get-tuple-element.21.where_slot, bf16[512,256]{1,0:T(8,128)(2,1)S(1)} %copy-done.1, ...), custom_call_target="tpu_custom_call" | custom-call | flops 1073741824 | bytes 4457348 | tf_op jit(solution)/shard_map/pallas_call | solution.py:33
  50.7 0.8 copy-done.10
  51.4 0.7 add.19
  52.1 1.6 %collective-permute-start.9 = (f32[136,256]{1,0:T(8,128)}, f32[136,256]{1,0:T(8,128)}, u32[]{:S(2)}, u32[]{:S(2)}) collective-permute-start(f32[136,256]{1,0:T(8,128)} %add.19), channel_id=1, source_target_pairs={{0,8},{1,17},{2,10},{3,19},{4,12},{5,21},{6,14},{7,23},{8,0},{9,25... | collective-permute-start | bytes 417800 | tf_op jit(solution)/shard_map/ppermute | solution.py:380
  53.7 0.7 slice.26
  54.4 1.5 %collective-permute-start.4 = (f32[24,16,256]{2,1,0:T(8,128)}, f32[24,16,256]{2,1,0:T(8,128)S(1)}, u32[]{:S(2)}, u32[]{:S(2)}) collective-permute-start(f32[24,16,256]{2,1,0:T(8,128)} %copy-done.10), channel_id=1, source_target_pairs={{0,2},{1,3},{2,0},{3,1},{4,6},{5,7},{6,4},{7,5},{8,10},{9,11},{10,... | collective-permute-start | bytes 1179656 | tf_op jit(solution)/shard_map/ppermute | solution.py:383
  55.9 1.1 %collective-permute-start.5 = (f32[24,16,256]{2,1,0:T(8,128)S(1)}, f32[24,16,256]{2,1,0:T(8,128)S(1)}, u32[]{:S(2)}, u32[]{:S(2)}) collective-permute-start(f32[24,16,256]{2,1,0:T(8,128)S(1)} %get-tuple-element.30), channel_id=1, source_target_pairs={{0,3},{1,2},{2,1},{3,0},{4,7},{5,6},{6,5},{7,4},{8,11},{9,10},{10,... | collective-permute-start | bytes 1179656 | tf_op jit(solution)/shard_map/ppermute | solution.py:383
  57.0 1.9 %collective-permute-done.9 = f32[136,256]{1,0:T(8,128)} collective-permute-done((f32[136,256]{1,0:T(8,128)}, f32[136,256]{1,0:T(8,128)}, u32[]{:S(2)}, u32[]{:S(2)}) %collective-permute-start.9) | collective-permute-done | bytes 139296 | tf_op jit(solution)/shard_map/ppermute | solution.py:380
  58.9 1.0 %add.20 = f32[136,256]{1,0:T(8,128)S(1)} add(f32[136,256]{1,0:T(8,128)} %add.19, f32[136,256]{1,0:T(8,128)} %collective-permute-done.9) | non-fusion elementwise | flops 34816 | bytes 417792 | tf_op jit(solution)/shard_map/add | solution.py:403
  59.9 2.2 %collective-permute-start.10 = (f32[136,256]{1,0:T(8,128)S(1)}, f32[136,256]{1,0:T(8,128)S(1)}, u32[]{:S(2)}, u32[]{:S(2)}) collective-permute-start(f32[136,256]{1,0:T(8,128)S(1)} %add.20), channel_id=1, source_target_pairs={{0,16},{1,9},{2,18},{3,11},{4,20},{5,13},{6,22},{7,15},{8,24},{9,1... | collective-permute-start | bytes 417800 | tf_op jit(solution)/shard_map/ppermute | solution.py:380
  62.1 4.7 %collective-permute-done.10 = f32[136,256]{1,0:T(8,128)S(1)} collective-permute-done((f32[136,256]{1,0:T(8,128)S(1)}, f32[136,256]{1,0:T(8,128)S(1)}, u32[]{:S(2)}, u32[]{:S(2)}) %collective-permute-start.10) | collective-permute-done | bytes 139296 | tf_op jit(solution)/shard_map/ppermute | solution.py:380
  66.9 0.9 %collective-permute-start.12 = (f32[136,256]{1,0:T(8,128)S(1)}, f32[136,256]{1,0:T(8,128)S(1)}, u32[]{:S(2)}, u32[]{:S(2)}) collective-permute-start(f32[136,256]{1,0:T(8,128)S(1)} %add.21.mine), channel_id=1, source_target_pairs={{0,1},{1,0},{2,3},{3,2},{4,5},{5,4},{6,7},{7,6},{8,9},{9,8},{10,11... | collective-permute-start | bytes 417800 | tf_op jit(solution)/shard_map/ppermute | solution.py:380
  67.8 1.3 %collective-permute-start.11 = (f32[136,256]{1,0:T(8,128)S(1)}, f32[136,256]{1,0:T(8,128)S(1)}, u32[]{:S(2)}, u32[]{:S(2)}) collective-permute-start(f32[136,256]{1,0:T(8,128)S(1)} %add.21.mine), channel_id=1, source_target_pairs={{0,2},{1,5},{2,0},{3,7},{4,6},{5,1},{6,4},{7,3},{8,10},{9,13},{10,... | collective-permute-start | bytes 417800 | tf_op jit(solution)/shard_map/ppermute | solution.py:380
  69.1 6.2 %collective-permute-done.5.rest_2_ = f32[24,16,256]{2,1,0:T(8,128)S(1)} collective-permute-done((f32[24,16,256]{2,1,0:T(8,128)S(1)}, f32[24,16,256]{2,1,0:T(8,128)S(1)}, u32[]{:S(2)}, u32[]{:S(2)}) %collective-permute-start.5) | collective-permute-done | bytes 393248 | tf_op jit(solution)/shard_map/ppermute | solution.py:383
  75.3 2.4 %shard_map.99 = f32[128,16,256]{2,1,0:T(8,128)} custom-call(s32[64]{0:T(128)S(1)} %copy-done.7, s32[3,24]{1,0:T(4,128)S(1)} %maximum_convert_fusion.asked, f32[128,16,256]{2,1,0:T(8,128)S(1)} %get-tuple-element.27.own_in, f32[24,16,256]{2,1,0:T(8,128)S(1)} %collective-permute-done.3.rest_0_, f32[24,16,256]{2,1,0:T(8,128)S(1)} %collective-permute-done.4.rest_1_, ...), custom_call_target="tpu_custom_call" | custom-call | bytes 3277344 | tf_op jit(solution)/shard_map/pallas_call | solution.py:33
  78.0 0.9 %shard_map.101 = (f32[512,256]{1,0:T(8,128)}, f32[1,1]{1,0:T(1,128)}) custom-call(f32[136,256]{1,0:T(8,128)S(1)} %add.21.mine, f32[136,256]{1,0:T(8,128)S(1)} %collective-permute-done.11.far, f32[136,256]{1,0:T(8,128)S(1)} %collective-permute-done.12.theirs, f32[136,256]{1,0:T(8,128)S(1)} %collective-permute-done.13.theirs_far), custom_call_target="tpu_custom_call" | custom-call | bytes 557056 | tf_op jit(solution)/shard_map/pallas_call | solution.py:33
  (49 shorter events, 0.9 us)
Async XLA Ops:
  2.9 15.3 %collective-permute-start.1 = (bf16[65,16,256]{2,1,0:T(8,128)(2,1)}, bf16[65,16,256]{2,1,0:T(8,128)(2,1)S(1)}, u32[]{:S(2)}, u32[]{:S(2)}) collective-permute-start(bf16[65,16,256]{2,1,0:T(8,128)(2,1)} %shard_map.94), channel_id=1, source_target_pairs={{0,2},{1,3},{2,0},{3,1},{4,6},{5,7},{6,4},{7,5},{8,10},{9,11},{10,... | collective-permute-start | bytes 1597448 | tf_op jit(solution)/shard_map/ppermute | solution.py:324
  5.9 23.3 %collective-permute-start = (bf16[65,16,256]{2,1,0:T(8,128)(2,1)}, bf16[65,16,256]{2,1,0:T(8,128)(2,1)S(1)}, u32[]{:S(2)}, u32[]{:S(2)}) collective-permute-start(bf16[65,16,256]{2,1,0:T(8,128)(2,1)} %shard_map.94), channel_id=1, source_target_pairs={{0,1},{1,0},{2,3},{3,2},{4,5},{5,4},{6,7},{7,6},{8,9},{9,8},{10,11... | collective-permute-start | bytes 1597448 | tf_op jit(solution)/shard_map/ppermute | solution.py:324
  18.2 11.0 %copy-start.9 = (bf16[65,16,256]{2,1,0:T(8,128)(2,1)}, bf16[65,16,256]{2,1,0:T(8,128)(2,1)S(1)}, u32[]{:S(2)}) copy-start(bf16[65,16,256]{2,1,0:T(8,128)(2,1)S(1)} %collective-permute-done.1.rest_1_) | copy-start | bytes 1597444
  18.2 11.0 %collective-permute-start.2 = (bf16[65,16,256]{2,1,0:T(8,128)(2,1)S(1)}, bf16[65,16,256]{2,1,0:T(8,128)(2,1)S(1)}, u32[]{:S(2)}, u32[]{:S(2)}) collective-permute-start(bf16[65,16,256]{2,1,0:T(8,128)(2,1)S(1)} %collective-permute-done.1.rest_1_), channel_id=1, source_target_pairs={{0,1},{1,0},{2,3},{3,2},{4,5},{5,4},{6,7},{7,6},{8,9},{9,8},{10,11... | collective-permute-start | bytes 1597448 | tf_op jit(solution)/shard_map/ppermute | solution.py:324
  18.2 1.1 %copy-start = (bf16[512,256]{1,0:T(8,128)(2,1)S(1)}, bf16[512,256]{1,0:T(8,128)(2,1)}, u32[]{:S(2)}) copy-start(bf16[512,256]{1,0:T(8,128)(2,1)} %weight.7) | copy-start | bytes 786436
  19.3 1.2 %copy-start.2 = (bf16[2048,256]{1,0:T(8,128)(2,1)S(1)}, bf16[2048,256]{1,0:T(8,128)(2,1)}, u32[]{:S(2)}) copy-start(bf16[2048,256]{1,0:T(8,128)(2,1)} %feat.1) | copy-start | bytes 3145732
  20.5 0.7 copy-start.4
  21.2 0.7 copy-start.6
  21.9 0.9 %copy-start.11 = (s32[2048,10]{0,1:T(8,128)S(1)}, s32[2048,10]{0,1:T(8,128)}, u32[]{:S(2)}) copy-start(s32[2048,10]{0,1:T(8,128)} %param.11) | copy-start | bytes 245764
  22.8 0.7 copy-start.14
  23.5 5.8 %copy-start.1 = (bf16[512,256]{1,0:T(8,128)(2,1)S(1)}, bf16[512,256]{1,0:T(8,128)(2,1)}, u32[]{:S(2)}) copy-start(bf16[512,256]{1,0:T(8,128)(2,1)} %weight.7) | copy-start | bytes 786436
  23.5 5.8 %copy-start.3 = (bf16[2048,256]{1,0:T(8,128)(2,1)S(1)}, bf16[2048,256]{1,0:T(8,128)(2,1)}, u32[]{:S(2)}) copy-start(bf16[2048,256]{1,0:T(8,128)(2,1)} %feat.1) | copy-start | bytes 3145732
  23.5 5.8 %copy-start.5 = (s32[4,24]{1,0:T(4,128)S(1)}, s32[4,24]{1,0:T(4,128)}, u32[]{:S(2)}) copy-start(s32[4,24]{1,0:T(4,128)} %request.5) | copy-start | bytes 1156
  23.5 5.8 %copy-start.12 = (s32[2048,10]{0,1:T(8,128)S(1)}, s32[2048,10]{0,1:T(8,128)}, u32[]{:S(2)}) copy-start(s32[2048,10]{0,1:T(8,128)} %param.11) | copy-start | bytes 245764
  23.5 5.8 %copy-start.13 = (s32[2048,4]{0,1:T(4,128)S(1)}, s32[2048,4]{0,1:T(4,128)}, u32[]{:S(2)}) copy-start(s32[2048,4]{0,1:T(4,128)} %param.12) | copy-start | bytes 98308
  29.2 8.2 %copy-start.8 = (bf16[65,16,256]{2,1,0:T(8,128)(2,1)}, bf16[65,16,256]{2,1,0:T(8,128)(2,1)S(1)}, u32[]{:S(2)}) copy-start(bf16[65,16,256]{2,1,0:T(8,128)(2,1)S(1)} %collective-permute-done.2.rest_2_) | copy-start | bytes 1597444
  37.4 1.6 %collective-permute-start.6 = (f32[264,256]{1,0:T(8,128)S(1)}, f32[264,256]{1,0:T(8,128)S(1)}, u32[]{:S(2)}, u32[]{:S(2)}) collective-permute-start(f32[264,256]{1,0:T(8,128)S(1)} %get-tuple-element.32), channel_id=1, source_target_pairs={{0,1},{1,0},{2,3},{3,2},{4,5},{5,4},{6,7},{7,6},{8,9},{9,8},{10,11... | collective-permute-start | bytes 811016 | tf_op jit(solution)/shard_map/ppermute | solution.py:380
  39.0 5.1 %collective-permute-start.7 = (f32[136,256]{1,0:T(8,128)S(1)}, f32[136,256]{1,0:T(8,128)S(1)}, u32[]{:S(2)}, u32[]{:S(2)}) collective-permute-start(f32[136,256]{1,0:T(8,128)S(1)} %get-tuple-element.34), channel_id=1, source_target_pairs={{0,2},{1,5},{2,0},{3,7},{4,6},{5,1},{6,4},{7,3},{8,10},{9,13},{10,... | collective-permute-start | bytes 417800 | tf_op jit(solution)/shard_map/ppermute | solution.py:380
  44.2 7.3 %collective-permute-start.8 = (f32[136,256]{1,0:T(8,128)S(1)}, f32[136,256]{1,0:T(8,128)S(1)}, u32[]{:S(2)}, u32[]{:S(2)}) collective-permute-start(f32[136,256]{1,0:T(8,128)S(1)} %add.18), channel_id=1, source_target_pairs={{0,4},{1,3},{2,6},{3,1},{4,0},{5,7},{6,2},{7,5},{8,12},{9,11},{10,... | collective-permute-start | bytes 417800 | tf_op jit(solution)/shard_map/ppermute | solution.py:380
  47.0 22.1 %slice-start = ((bf16[65,16,256]{2,1,0:T(8,128)(2,1)}), bf16[1,16,256]{2,1,0:T(8,128)(2,1)S(1)}, s32[]{:S(2)}) async-start(bf16[65,16,256]{2,1,0:T(8,128)(2,1)} %copy-done.8), calls=%async_computation | async-start | bytes 16384 | tf_op jit(solution)/shard_map/slice | solution.py:418
  47.0 28.3 %copy-start.7 = (s32[64]{0:T(128)S(1)}, s32[64]{0:T(128)}, u32[]{:S(2)}) copy-start(s32[64]{0:T(128)} %boundary.5) | copy-start | bytes 772
  50.7 0.8 copy-start.10
  51.4 16.3 %collective-permute-start.3 = (f32[24,16,256]{2,1,0:T(8,128)}, f32[24,16,256]{2,1,0:T(8,128)S(1)}, u32[]{:S(2)}, u32[]{:S(2)}) collective-permute-start(f32[24,16,256]{2,1,0:T(8,128)} %get-tuple-element.28), channel_id=1, source_target_pairs={{0,1},{1,0},{2,3},{3,2},{4,5},{5,4},{6,7},{7,6},{8,9},{9,8},{10,11... | collective-permute-start | bytes 1179656 | tf_op jit(solution)/shard_map/ppermute | solution.py:383
  52.1 6.8 %collective-permute-start.9 = (f32[136,256]{1,0:T(8,128)}, f32[136,256]{1,0:T(8,128)}, u32[]{:S(2)}, u32[]{:S(2)}) collective-permute-start(f32[136,256]{1,0:T(8,128)} %add.19), channel_id=1, source_target_pairs={{0,8},{1,17},{2,10},{3,19},{4,12},{5,21},{6,14},{7,23},{8,0},{9,25... | collective-permute-start | bytes 417800 | tf_op jit(solution)/shard_map/ppermute | solution.py:380
  54.4 14.7 %collective-permute-start.4 = (f32[24,16,256]{2,1,0:T(8,128)}, f32[24,16,256]{2,1,0:T(8,128)S(1)}, u32[]{:S(2)}, u32[]{:S(2)}) collective-permute-start(f32[24,16,256]{2,1,0:T(8,128)} %copy-done.10), channel_id=1, source_target_pairs={{0,2},{1,3},{2,0},{3,1},{4,6},{5,7},{6,4},{7,5},{8,10},{9,11},{10,... | collective-permute-start | bytes 1179656 | tf_op jit(solution)/shard_map/ppermute | solution.py:383
  55.9 19.4 %collective-permute-start.5 = (f32[24,16,256]{2,1,0:T(8,128)S(1)}, f32[24,16,256]{2,1,0:T(8,128)S(1)}, u32[]{:S(2)}, u32[]{:S(2)}) collective-permute-start(f32[24,16,256]{2,1,0:T(8,128)S(1)} %get-tuple-element.30), channel_id=1, source_target_pairs={{0,3},{1,2},{2,1},{3,0},{4,7},{5,6},{6,5},{7,4},{8,11},{9,10},{10,... | collective-permute-start | bytes 1179656 | tf_op jit(solution)/shard_map/ppermute | solution.py:383
  59.9 7.0 %collective-permute-start.10 = (f32[136,256]{1,0:T(8,128)S(1)}, f32[136,256]{1,0:T(8,128)S(1)}, u32[]{:S(2)}, u32[]{:S(2)}) collective-permute-start(f32[136,256]{1,0:T(8,128)S(1)} %add.20), channel_id=1, source_target_pairs={{0,16},{1,9},{2,18},{3,11},{4,20},{5,13},{6,22},{7,15},{8,24},{9,1... | collective-permute-start | bytes 417800 | tf_op jit(solution)/shard_map/ppermute | solution.py:380
  66.8 10.9 %collective-permute-start.13 = (f32[136,256]{1,0:T(8,128)S(1)}, f32[136,256]{1,0:T(8,128)S(1)}, u32[]{:S(2)}, u32[]{:S(2)}) collective-permute-start(f32[136,256]{1,0:T(8,128)S(1)} %add.21.mine), channel_id=1, source_target_pairs={{0,3},{1,4},{2,1},{3,6},{4,7},{5,0},{6,5},{7,2},{8,11},{9,12},{10,... | collective-permute-start | bytes 417800 | tf_op jit(solution)/shard_map/ppermute | solution.py:380
  66.9 10.8 %collective-permute-start.12 = (f32[136,256]{1,0:T(8,128)S(1)}, f32[136,256]{1,0:T(8,128)S(1)}, u32[]{:S(2)}, u32[]{:S(2)}) collective-permute-start(f32[136,256]{1,0:T(8,128)S(1)} %add.21.mine), channel_id=1, source_target_pairs={{0,1},{1,0},{2,3},{3,2},{4,5},{5,4},{6,7},{7,6},{8,9},{9,8},{10,11... | collective-permute-start | bytes 417800 | tf_op jit(solution)/shard_map/ppermute | solution.py:380
  67.8 10.2 %collective-permute-start.11 = (f32[136,256]{1,0:T(8,128)S(1)}, f32[136,256]{1,0:T(8,128)S(1)}, u32[]{:S(2)}, u32[]{:S(2)}) collective-permute-start(f32[136,256]{1,0:T(8,128)S(1)} %add.21.mine), channel_id=1, source_target_pairs={{0,2},{1,5},{2,0},{3,7},{4,6},{5,1},{6,4},{7,3},{8,10},{9,13},{10,... | collective-permute-start | bytes 417800 | tf_op jit(solution)/shard_map/ppermute | solution.py:380
